TPU v7x, 32 devices: a whole 2x2x4 slice. The times are simulated.
32 devices in a mesh: clip: 4 (over y, x), tm: 4 (over z), space: 2 (over core).
Axes of the slice: x: 2, y: 2, z: 4, core: 2. Of those that a mesh axis runs over, the one named last changes fastest.
Arguments:
- latents: bfloat16 [8, 8, 4, 64, 384], P('clip', 'tm', 'space'), parts along dimension 0, may hold values from -6 to 6
- frame_counts: int32 [8], P('clip'), parts along dimension 0, may hold values from 1 to 8, as said below
- norm_gain: float32 [384], replicated, may hold values from 0.1 to 1.9
- norm_bias: float32 [384], replicated, may hold values from -3 to 3
- conv3_weight: bfloat16 [3, 3, 3, 384, 384], replicated, may hold values from -0.0625 to 0.0625
- conv3_bias: float32 [384], replicated, may hold values from -3 to 3
- conv2_weight: bfloat16 [3, 3, 384, 384], replicated, may hold values from -0.109375 to 0.109375
- conv2_bias: float32 [384], replicated, may hold values from -3 to 3
Outputs:
- decoded: bfloat16 [8, 8, 8, 128, 384], P('clip', 'tm', 'space'), parts along dimension 0
There are 4 independent parts, one for each index of `clip`. A program takes and returns all parts, laid end to end along the dimension named above; an argument that names none is the same for every part. Nothing has to cross between parts.
Inputs may be any that keep to these rules, and one draw needn't show every extreme that they name: `frame_counts`: each clip has between 1 and 8 real frames; in every draw some clip has all 8.
All inputs are finite; a program needn't handle non-finite values.
Results may differ from a plain program's by a relative error of at most 0.0051.
Values may be sent and summed in bfloat16 or wider, within the bound.
No kernel may reach another device: no remote copies, remote signals or barrier semaphores. Data moves between devices by JAX's collectives and lax.ppermute only.
A program may use at most 64 MiB of HBM per device.

v0:
```python
import jax
import jax.numpy as jnp
from jax import lax
from jax.sharding import PartitionSpec as P

GROUPS = 32


epsilon = 1e-05


def extended(cells, sides, width):
    for axis, dim in sides:
        count = lax.axis_size(axis)
        ends = count - 1
        head = lax.slice_in_dim(cells, 0, width, axis=dim)
        tail = lax.slice_in_dim(cells, cells.shape[dim] - width, cells.shape[dim], axis=dim)
        cells = jnp.concatenate(
            [
                lax.ppermute(tail, axis, [(i, (i + 1) % count) for i in range(ends)]),
                cells,
                lax.ppermute(head, axis, [((i + 1) % count, i) for i in range(ends)]),
            ],
            axis=dim,
        )
    return cells


def from_behind(value, axis, steps):
    count = lax.axis_size(axis)
    first, last = (max(0, -steps), min(count, count - steps))
    return lax.ppermute(value, axis, [(source, source + steps) for source in range(first, last)])


def conv_volume(stacked, kernel):
    return lax.conv_general_dilated(
        stacked,
        kernel,
        (1, 1, 1),
        ((0, 0), (0, 0), (1, 1)),
        dimension_numbers=("NDHWC", "DHWIO", "NDHWC"),
        preferred_element_type=jnp.float32,
    )


def per_clip(section_fn, inputs, live_clip, out_shape):
    results = []
    for clip_index in range(inputs[0].shape[0]):
        pieces = tuple((item[clip_index : clip_index + 1] for item in inputs))
        results.append(
            lax.cond(
                live_clip[clip_index],
                lambda group: section_fn(*group),
                lambda group: jnp.zeros(out_shape, jnp.bfloat16),
                pieces,
            )
        )
    return jnp.concatenate(results, axis=0)


def body(
    latents, frame_counts, norm_gain, norm_bias, conv3_weight, conv3_bias, conv2_weight, conv2_bias
):
    clips, frames_dev, rows_dev, columns, channels = latents.shape
    per_group = channels // GROUPS
    total_rows = rows_dev * lax.axis_size("space")
    frame_ids = lax.axis_index("tm") * frames_dev + jnp.arange(frames_dev, dtype=jnp.int32)
    frame_mask = (frame_ids[None, :] < frame_counts[:, None]).astype(jnp.float32)
    broad_mask = frame_mask[:, :, None, None, None]
    live_clip = jnp.sum(frame_mask, axis=1) > 0.0
    values = latents.astype(jnp.float32)
    grouped = (values * broad_mask).reshape(clips, frames_dev, rows_dev, columns, GROUPS, per_group)
    first = jnp.sum(grouped, axis=(1, 2, 3, 5))
    second = jnp.sum(grouped * grouped, axis=(1, 2, 3, 5))
    total_first, total_second = lax.psum((first, second), ("tm", "space"))
    cells = (frame_counts * (total_rows * columns * per_group)).astype(jnp.float32)[:, None]
    mean = total_first / cells
    variance = total_second / cells - mean * mean
    scale = lax.rsqrt(variance + epsilon)
    mean_ch = jnp.repeat(mean, per_group, axis=1)[:, None, None, None, :]
    scale_ch = jnp.repeat(scale, per_group, axis=1)[:, None, None, None, :]
    shifted = (latents.astype(jnp.float32) - mean_ch) * scale_ch * norm_gain + norm_bias
    activated = (jax.nn.silu(shifted) * broad_mask).astype(jnp.bfloat16)
    activated = extended(activated, (("space", 2),), 1)
    earlier = from_behind(activated, "tm", 1)
    stacked = jnp.concatenate([earlier, activated], axis=1)

    def block_section(stacked_part, resid_part, mask_part):
        convolved = conv_volume(stacked_part, conv3_weight)
        return ((resid_part.astype(jnp.float32) + convolved + conv3_bias) * mask_part).astype(
            jnp.bfloat16
        )

    middle_rows = latents.shape[2]
    middle = per_clip(
        block_section,
        (stacked, latents, broad_mask),
        live_clip,
        (1, frames_dev, middle_rows, columns, channels),
    )
    middle = extended(middle, (("space", 2),), 1)

    def planar_section(middle_part, mask_part):
        count = middle_part.shape[0]
        upsampled = jnp.repeat(jnp.repeat(middle_part, 2, axis=2), 2, axis=3)[:, :, 1:-1]
        flat = upsampled.reshape(count * frames_dev, 2 * rows_dev + 2, 2 * columns, channels)
        planar = lax.conv_general_dilated(
            flat,
            conv2_weight,
            (1, 1),
            ((0, 0), (1, 1)),
            dimension_numbers=("NHWC", "HWIO", "NHWC"),
            preferred_element_type=jnp.float32,
        )
        planar = planar.reshape(count, frames_dev, 2 * rows_dev, 2 * columns, channels)
        return ((planar + conv2_bias) * mask_part).astype(jnp.bfloat16)

    return per_clip(
        planar_section,
        (middle, broad_mask),
        live_clip,
        (1, frames_dev, 2 * rows_dev, 2 * columns, channels),
    )


def solution(mesh):
    placed = (P("clip", "tm", "space", None, None), P("clip"), P(), P(), P(), P(), P(), P())
    return jax.shard_map(
        body,
        mesh=mesh,
        in_specs=placed,
        out_specs=P("clip", "tm", "space", None, None),
        check_vma=False,
    )
```

profile of v0, /device:TPU:0, one launch (start us, length us, event | category | flops | bytes accessed | tf_op | source)
XLA Modules:
  0.0 91.1 jit_solution(17409547976832938428)
XLA Ops:
  1.4 1.2 %fusion.40 = (f32[2,384]{1,0:T(2,128)S(1)}, f32[2,384]{1,0:T(2,128)S(1)}) fusion(bf16[2,2,2,64,384]{4,3,2,1,0:T(8,128)(2,1)} %param.16, f32[2,2]{1,0:T(2,128)S(1)} %compare_convert_fusion), kind=kLoop, calls=%fused_computation.60 | loop fusion | flops 981504 | bytes 399376 | tf_op jit(solution)/shard_map/reduce_sum | solution.py:74
  3.0 18.1 %all-reduce = (f32[2,32]{1,0:T(2,128)S(1)}, f32[2,32]{1,0:T(2,128)S(1)}) all-reduce(f32[2,32]{1,0:T(2,128)S(1)} %reduce_sum.44, f32[2,32]{1,0:T(2,128)S(1)} %reduce_sum.47), channel_id=1, replica_groups=mesh['clip'=4,'tm'=4,'space'=2] {'tm','space'}, use_global_device_ids=true, to_apply=%region_3.0 | all-reduce | flops 128 | bytes 1024 | tf_op jit(solution)/shard_map/psum | solution.py:75
  21.6 1.3 %fusion.50 = bf16[2,2,2,64,384]{4,3,2,1,0:T(8,128)(2,1)S(1)} fusion(bf16[2,2,2,64,384]{4,3,2,1,0:T(8,128)(2,1)} %param.16, f32[384]{0:T(512)} %param.19, f32[384]{0:T(512)} %param.18, f32[2,384]{1,0:T(2,128)S(1)} %mul.97, f32[2,384]{1,0:T(2,128)S(1)} %sub.13, f32[2,2]{1,0:T(2,128)S(1)} %compare_convert_fusion), kind=kLoop, calls=%fused_computation.70 | loop fusion | flops 2162688 | bytes 795664 | tf_op jit(solution)/shard_map/convert_element_type | solution.py:83
  22.9 1.3 %collective-permute-start = (bf16[2,2,1,64,384]{4,3,2,1,0:T(8,128)(2,1)S(1)}, bf16[2,2,1,64,384]{4,3,2,1,0:T(8,128)(2,1)S(1)}, u32[]{:S(2)}, u32[]{:S(2)}) collective-permute-start(bf16[2,2,1,64,384]{4,3,2,1,0:T(8,128)(2,1)S(1)} %get-tuple-element.109), channel_id=1, source_target_pairs={{0,1},{2,3},{4,5},{6,7},{8,9},{10,11},{12,13},{14,15},{16,17},{18,... | collective-permute-start | bytes 589832 | tf_op jit(solution)/shard_map/ppermute | solution.py:20
  24.3 1.3 %collective-permute-start.1 = (bf16[2,2,1,64,384]{4,3,2,1,0:T(8,128)(2,1)S(1)}, bf16[2,2,1,64,384]{4,3,2,1,0:T(8,128)(2,1)S(1)}, u32[]{:S(2)}, u32[]{:S(2)}) collective-permute-start(bf16[2,2,1,64,384]{4,3,2,1,0:T(8,128)(2,1)S(1)} %get-tuple-element.110), channel_id=1, source_target_pairs={{1,0},{3,2},{5,4},{7,6},{9,8},{11,10},{13,12},{15,14},{17,16},{19,... | collective-permute-start | bytes 589832 | tf_op jit(solution)/shard_map/ppermute | solution.py:22
  25.6 2.0 %collective-permute-done.1 = bf16[2,2,1,64,384]{4,3,2,1,0:T(8,128)(2,1)S(1)} collective-permute-done((bf16[2,2,1,64,384]{4,3,2,1,0:T(8,128)(2,1)S(1)}, bf16[2,2,1,64,384]{4,3,2,1,0:T(8,128)(2,1)S(1)}, u32[]{:S(2)}, u32[]{:S(2)}) %collective-permute-start.1) | collective-permute-done | bytes 196640 | tf_op jit(solution)/shard_map/ppermute | solution.py:22
  27.7 1.3 %collective-permute-start.2 = (bf16[2,2,4,64,384]{4,3,2,1,0:T(8,128)(2,1)S(1)}, bf16[2,2,4,64,384]{4,3,2,1,0:T(8,128)(2,1)S(1)}, u32[]{:S(2)}, u32[]{:S(2)}) collective-permute-start(bf16[2,2,4,64,384]{4,3,2,1,0:T(8,128)(2,1)S(1)} %pad_maximum_fusion.1), channel_id=1, source_target_pairs={{0,2},{2,4},{4,6},{1,3},{3,5},{5,7},{8,10},{10,12},{12,14},{9,11},... | collective-permute-start | bytes 2359304 | tf_op jit(solution)/shard_map/ppermute | solution.py:32
  31.2 15.2 %collective-permute-done.2 = bf16[2,2,4,64,384]{4,3,2,1,0:T(8,128)(2,1)S(1)} collective-permute-done((bf16[2,2,4,64,384]{4,3,2,1,0:T(8,128)(2,1)S(1)}, bf16[2,2,4,64,384]{4,3,2,1,0:T(8,128)(2,1)S(1)}, u32[]{:S(2)}, u32[]{:S(2)}) %collective-permute-start.2) | collective-permute-done | bytes 786464 | tf_op jit(solution)/shard_map/ppermute | solution.py:32
  46.6 7.8 %conditional.4 = (bf16[1,2,2,64,384]{4,1,3,2,0:T(2,128)(2,1)S(1)}) conditional(s32[]{:T(128)} %bitcast.40, () %tuple.30, (bf16[2,2,2,64,384]{4,3,2,1,0:T(8,128)(2,1)S(1)}, bf16[2,4,4,64,384]{4,3,2,1,0:T(8,128)(2,1)S(1)}, bf16[3,3,3,384,384]{4,3,2,1,0:T(8,128)(2,1)}, f32[384]{0:T(512)S(1)}, f32[1,2,1,1,1]{1,4,3,2,0:T(1,128)S(1)}) %tuple.65), branch_computations={%region_7.8_spmd, %region_8.9_spmd} | conditional | flops 2297081856 | bytes 52668340 | solution.py:51
  47.1 1.2 %copy.43 = bf16[2,4,4,64,384]{4,2,3,1,0:T(4,128)(2,1)S(1)} copy(bf16[2,4,4,64,384]{4,3,2,1,0:T(8,128)(2,1)S(1)} %get-tuple-element.88) | data formatting | bytes 3145728 | tf_op jit(solution)/shard_map
  49.1 1.2 %copy-done.3 = bf16[3,3,3,384,384]{4,3,2,1,0:T(8,128)(2,1)S(1)} copy-done((bf16[3,3,3,384,384]{4,3,2,1,0:T(8,128)(2,1)S(1)}, bf16[3,3,3,384,384]{4,3,2,1,0:T(8,128)(2,1)}, u32[]{:S(2)}) %copy-start.3) | copy-done | bytes 7962648 | tf_op jit(solution)/shard_map/cond
  50.3 3.4 %convolution_select_fusion = f32[2,2,8,9,384]{4,2,3,1,0:T(8,128)S(1)} fusion(bf16[3,3,3,384,384]{4,3,2,1,0:T(8,128)(2,1)S(1)} %copy-done.3, bf16[4,4,1,7,2,384]{5,3,4,1,0,2:T(8,128)(2,1)S(1)} %slice.84, bf16[4,4,1,8,9,384]{5,3,4,1,0,2:T(8,128)(2,1)S(1)} %copy.31, pred[8,9]{0,1:T(8,128)(4,1)S(1)} %copy-done.10), kind=kOutput, calls=%fused_computation.2 | convolution fusion | flops 2296590336 | bytes 9461832 | tf_op jit(solution)/shard_map/cond/branch_1_fun/conv_general_dilated | solution.py:36
  54.6 8.0 %conditional.5 = (bf16[1,2,2,64,384]{4,1,3,2,0:T(2,128)(2,1)S(1)}) conditional(s32[]{:T(128)} %bitcast.42, () %tuple.32, (bf16[2,2,2,64,384]{4,3,2,1,0:T(8,128)(2,1)S(1)}, bf16[2,4,4,64,384]{4,3,2,1,0:T(8,128)(2,1)S(1)}, bf16[3,3,3,384,384]{4,3,2,1,0:T(8,128)(2,1)}, f32[384]{0:T(512)S(1)}, f32[1,2,1,1,1]{1,4,3,2,0:T(1,128)S(1)}) %tuple.66), branch_computations={%region_9.10_spmd, %region_10.11_spmd} | conditional | flops 2297081856 | bytes 52668340 | solution.py:51
  55.2 1.2 %copy.45 = bf16[2,4,4,64,384]{4,2,3,1,0:T(4,128)(2,1)S(1)} copy(bf16[2,4,4,64,384]{4,3,2,1,0:T(8,128)(2,1)S(1)} %get-tuple-element.93) | data formatting | bytes 3145728 | tf_op jit(solution)/shard_map
  57.2 1.2 %copy-done.4 = bf16[3,3,3,384,384]{4,3,2,1,0:T(8,128)(2,1)S(1)} copy-done((bf16[3,3,3,384,384]{4,3,2,1,0:T(8,128)(2,1)S(1)}, bf16[3,3,3,384,384]{4,3,2,1,0:T(8,128)(2,1)}, u32[]{:S(2)}) %copy-start.4) | copy-done | bytes 7962648 | tf_op jit(solution)/shard_map/cond
  58.4 3.4 %convolution_select_fusion.1 = f32[2,2,8,9,384]{4,2,3,1,0:T(8,128)S(1)} fusion(bf16[3,3,3,384,384]{4,3,2,1,0:T(8,128)(2,1)S(1)} %copy-done.4, bf16[4,4,1,7,2,384]{5,3,4,1,0,2:T(8,128)(2,1)S(1)} %slice.88, bf16[4,4,1,8,9,384]{5,3,4,1,0,2:T(8,128)(2,1)S(1)} %copy.34, pred[8,9]{0,1:T(8,128)(4,1)S(1)} %copy-done.11), kind=kOutput, calls=%fused_computation.20 | convolution fusion | flops 2296590336 | bytes 9461832 | tf_op jit(solution)/shard_map/cond/branch_1_fun/conv_general_dilated | solution.py:36
  63.1 1.6 %collective-permute-start.3 = (bf16[2,2,1,64,384]{4,1,3,2,0:T(2,128)(2,1)S(1)}, bf16[2,2,1,64,384]{4,1,3,2,0:T(2,128)(2,1)S(1)}, u32[]{:S(2)}, u32[]{:S(2)}) collective-permute-start(bf16[2,2,1,64,384]{4,1,3,2,0:T(2,128)(2,1)S(1)} %get-tuple-element.107), channel_id=1, source_target_pairs={{0,1},{2,3},{4,5},{6,7},{8,9},{10,11},{12,13},{14,15},{16,17},{18,... | collective-permute-start | bytes 589832 | tf_op jit(solution)/shard_map/ppermute | solution.py:20
  64.7 1.3 %collective-permute-start.4 = (bf16[2,2,1,64,384]{4,1,3,2,0:T(2,128)(2,1)S(1)}, bf16[2,2,1,64,384]{4,1,3,2,0:T(2,128)(2,1)S(1)}, u32[]{:S(2)}, u32[]{:S(2)}) collective-permute-start(bf16[2,2,1,64,384]{4,1,3,2,0:T(2,128)(2,1)S(1)} %get-tuple-element.108), channel_id=1, source_target_pairs={{1,0},{3,2},{5,4},{7,6},{9,8},{11,10},{13,12},{15,14},{17,16},{19,... | collective-permute-start | bytes 589832 | tf_op jit(solution)/shard_map/ppermute | solution.py:22
  66.0 2.0 %collective-permute-done.4 = bf16[2,2,1,64,384]{4,1,3,2,0:T(2,128)(2,1)S(1)} collective-permute-done((bf16[2,2,1,64,384]{4,1,3,2,0:T(2,128)(2,1)S(1)}, bf16[2,2,1,64,384]{4,1,3,2,0:T(2,128)(2,1)S(1)}, u32[]{:S(2)}, u32[]{:S(2)}) %collective-permute-start.4) | collective-permute-done | bytes 196640 | tf_op jit(solution)/shard_map/ppermute | solution.py:22
  68.0 1.2 %pad_maximum_fusion.2 = bf16[2,2,4,64,384]{4,1,3,2,0:T(2,128)(2,1)S(1)} fusion(bf16[2,2,1,64,384]{4,1,3,2,0:T(2,128)(2,1)S(1)} %collective-permute-done.4, bf16[2,2,2,64,384]{4,1,3,2,0:T(2,128)(2,1)S(1)} %constant_dynamic-update-slice_fusion, bf16[2,2,1,64,384]{4,1,3,2,0:T(2,128)(2,1)S(1)} %collective-permute-done.3), kind=kLoop, calls=%fused_computation.72 | loop fusion | flops 786432 | bytes 1572864 | tf_op jit(solution)/shard_map/concatenate | solution.py:18
  69.2 10.2 %conditional.6 = (bf16[1,2,4,128,384]{4,3,2,1,0:T(8,128)(2,1)S(1)}) conditional(s32[]{:T(128)} %bitcast.40, () %tuple.29, (bf16[2,2,4,64,384]{4,1,3,2,0:T(2,128)(2,1)S(1)}, bf16[3,3,384,384]{3,2,1,0:T(8,128)(2,1)S(1)}, f32[384]{0:T(512)S(1)}, f32[1,2,1,1,1]{1,4,3,2,0:T(1,128)S(1)}) %tuple.68), branch_computations={%region_11.12_spmd, %region_12.13_spmd} | conditional | flops 2893651968 | bytes 25211774 | solution.py:51
  70.2 0.8 broadcast_in_dim.10
  71.0 0.8 slice_bitcast_fusion.4
  71.8 0.9 %pad.4 = bf16[6,2,136,384]{3,1,2,0:T(2,128)(2,1)S(1)} pad(bf16[6,2,128,384]{3,1,2,0:T(2,128)(2,1)S(1)} %slice_bitcast_fusion.4, bf16[]{:T(256)} %constant.36), padding=0_0x0_0x1_7x0_0 | pad | bytes 2433026 | tf_op jit(solution)/shard_map/cond/branch_1_fun/reshape | solution.py:106
  72.9 1.3 %fusion.31 = bf16[6,2,8,19,384]{4,1,3,2,0:T(2,128)(2,1)S(1)} fusion(bf16[6,2,7,2,384]{4,1,3,2,0:T(2,128)(2,1)S(1)} %slice.91, bf16[6,2,8,17,384]{4,1,3,2,0:T(2,128)(2,1)S(1)} %bitcast.85), kind=kLoop, calls=%fused_computation.39 | loop fusion | flops 4202496 | bytes 2783232 | tf_op jit(solution)/shard_map/cond/branch_1_fun/conv_general_dilated | solution.py:107
  74.5 4.2 %fusion.30 = bf16[4,16,17,384]{3,1,2,0:T(8,128)(2,1)S(1)} fusion(f32[4,16,17,384]{3,0,2,1:T(4,128)S(1)} %bitcast.96, bf16[3,3,384,384]{3,2,1,0:T(8,128)(2,1)S(1)} %get-tuple-element.70, bf16[6,2,8,19,384]{4,1,3,2,0:T(2,128)(2,1)S(1)} %fusion.31, f32[384]{0:T(512)S(1)} %get-tuple-element.71, pred[16,17]{0,1:T(8,128)(4,1)S(1)} %copy-done.8), kind=kOutput, calls=%fused_computation.38 | convolution fusion | flops 2889449472 | bytes 6563600 | tf_op jit(solution)/shard_map/cond/branch_1_fun/conv_general_dilated | solution.py:107
  79.4 10.3 %conditional.7 = (bf16[1,2,4,128,384]{4,3,2,1,0:T(8,128)(2,1)S(1)}) conditional(s32[]{:T(128)} %bitcast.42, () %tuple.35, (bf16[2,2,4,64,384]{4,1,3,2,0:T(2,128)(2,1)S(1)}, bf16[3,3,384,384]{3,2,1,0:T(8,128)(2,1)}, f32[384]{0:T(512)S(1)}, f32[1,2,1,1,1]{1,4,3,2,0:T(1,128)S(1)}) %tuple.69), branch_computations={%region_13.14_spmd, %region_14.15_spmd} | conditional | flops 2893651968 | bytes 35828632 | solution.py:51
  80.4 0.8 broadcast_in_dim.32
  82.0 0.9 %pad.6 = bf16[6,2,136,384]{3,1,2,0:T(2,128)(2,1)S(1)} pad(bf16[6,2,128,384]{3,1,2,0:T(2,128)(2,1)S(1)} %slice_bitcast_fusion.7, bf16[]{:T(256)} %constant.40), padding=0_0x0_0x1_7x0_0 | pad | bytes 2433026 | tf_op jit(solution)/shard_map/cond/branch_1_fun/reshape | solution.py:106
  83.1 1.3 %fusion.35 = bf16[6,2,8,19,384]{4,1,3,2,0:T(2,128)(2,1)S(1)} fusion(bf16[6,2,7,2,384]{4,1,3,2,0:T(2,128)(2,1)S(1)} %slice.94, bf16[6,2,8,17,384]{4,1,3,2,0:T(2,128)(2,1)S(1)} %bitcast.87), kind=kLoop, calls=%fused_computation.48 | loop fusion | flops 4202496 | bytes 2783232 | tf_op jit(solution)/shard_map/cond/branch_1_fun/conv_general_dilated | solution.py:107
  84.9 4.2 %fusion.34 = bf16[4,16,17,384]{3,1,2,0:T(8,128)(2,1)S(1)} fusion(f32[4,16,17,384]{3,0,2,1:T(4,128)S(1)} %bitcast.97, bf16[3,3,384,384]{3,2,1,0:T(8,128)(2,1)S(1)} %copy-done.6, bf16[6,2,8,19,384]{4,1,3,2,0:T(2,128)(2,1)S(1)} %fusion.35, f32[384]{0:T(512)S(1)} %get-tuple-element.75, pred[16,17]{0,1:T(8,128)(4,1)S(1)} %copy-done.9), kind=kOutput, calls=%fused_computation.47 | convolution fusion | flops 2889449472 | bytes 6563600 | tf_op jit(solution)/shard_map/cond/branch_1_fun/conv_general_dilated | solution.py:107
  89.8 1.3 %pad_maximum_fusion = bf16[2,2,4,128,384]{4,3,2,1,0:T(8,128)(2,1)} fusion(bf16[1,2,4,128,384]{4,3,2,1,0:T(8,128)(2,1)S(1)} %get-tuple-element.100, bf16[1,2,4,128,384]{4,3,2,1,0:T(8,128)(2,1)S(1)} %get-tuple-element.99), kind=kLoop, calls=%fused_computation.55 | loop fusion | flops 786432 | bytes 3145728 | tf_op jit(solution)/shard_map/concatenate | solution.py:58
  (77 shorter events, 12.3 us)
Async XLA Ops:
  21.5 7.5 %copy-start.2 = (s32[2]{0:T(128)S(1)}, s32[2]{0:T(128)}, u32[]{:S(2)}) copy-start(s32[2]{0:T(128)} %param.17) | copy-start | bytes 28
  22.9 2.6 %collective-permute-start = (bf16[2,2,1,64,384]{4,3,2,1,0:T(8,128)(2,1)S(1)}, bf16[2,2,1,64,384]{4,3,2,1,0:T(8,128)(2,1)S(1)}, u32[]{:S(2)}, u32[]{:S(2)}) collective-permute-start(bf16[2,2,1,64,384]{4,3,2,1,0:T(8,128)(2,1)S(1)} %get-tuple-element.109), channel_id=1, source_target_pairs={{0,1},{2,3},{4,5},{6,7},{8,9},{10,11},{12,13},{14,15},{16,17},{18,... | collective-permute-start | bytes 589832 | tf_op jit(solution)/shard_map/ppermute | solution.py:20
  24.3 3.3 %collective-permute-start.1 = (bf16[2,2,1,64,384]{4,3,2,1,0:T(8,128)(2,1)S(1)}, bf16[2,2,1,64,384]{4,3,2,1,0:T(8,128)(2,1)S(1)}, u32[]{:S(2)}, u32[]{:S(2)}) collective-permute-start(bf16[2,2,1,64,384]{4,3,2,1,0:T(8,128)(2,1)S(1)} %get-tuple-element.110), channel_id=1, source_target_pairs={{1,0},{3,2},{5,4},{7,6},{9,8},{11,10},{13,12},{15,14},{17,16},{19,... | collective-permute-start | bytes 589832 | tf_op jit(solution)/shard_map/ppermute | solution.py:22
  27.7 18.7 %collective-permute-start.2 = (bf16[2,2,4,64,384]{4,3,2,1,0:T(8,128)(2,1)S(1)}, bf16[2,2,4,64,384]{4,3,2,1,0:T(8,128)(2,1)S(1)}, u32[]{:S(2)}, u32[]{:S(2)}) collective-permute-start(bf16[2,2,4,64,384]{4,3,2,1,0:T(8,128)(2,1)S(1)} %pad_maximum_fusion.1), channel_id=1, source_target_pairs={{0,2},{2,4},{4,6},{1,3},{3,5},{5,7},{8,10},{10,12},{12,14},{9,11},... | collective-permute-start | bytes 2359304 | tf_op jit(solution)/shard_map/ppermute | solution.py:32
  31.2 15.4 %copy-start = (bf16[2,2,2,64,384]{4,3,2,1,0:T(8,128)(2,1)S(1)}, bf16[2,2,2,64,384]{4,3,2,1,0:T(8,128)(2,1)}, u32[]{:S(2)}) copy-start(bf16[2,2,2,64,384]{4,3,2,1,0:T(8,128)(2,1)} %param.16) | copy-start | bytes 1179652
  31.2 15.4 %copy-start.1 = (f32[384]{0:T(512)S(1)}, f32[384]{0:T(512)}, u32[]{:S(2)}) copy-start(f32[384]{0:T(512)} %param.21) | copy-start | bytes 4612
  47.0 3.3 %copy-start.3 = (bf16[3,3,3,384,384]{4,3,2,1,0:T(8,128)(2,1)S(1)}, bf16[3,3,3,384,384]{4,3,2,1,0:T(8,128)(2,1)}, u32[]{:S(2)}) copy-start(bf16[3,3,3,384,384]{4,3,2,1,0:T(8,128)(2,1)} %get-tuple-element.61) | copy-start | bytes 23887876 | tf_op jit(solution)/shard_map/cond
  48.6 1.7 %copy-start.10 = (pred[8,9]{0,1:T(8,128)(4,1)S(1)}, pred[8,9]{0,1:T(8,128)(4,1)}, u32[]{:S(2)}) copy-start(pred[8,9]{0,1:T(8,128)(4,1)} %constant.47) | copy-start | bytes 220 | tf_op jit(solution)/shard_map/cond
  55.2 3.3 %copy-start.4 = (bf16[3,3,3,384,384]{4,3,2,1,0:T(8,128)(2,1)S(1)}, bf16[3,3,3,384,384]{4,3,2,1,0:T(8,128)(2,1)}, u32[]{:S(2)}) copy-start(bf16[3,3,3,384,384]{4,3,2,1,0:T(8,128)(2,1)} %get-tuple-element.66) | copy-start | bytes 23887876 | tf_op jit(solution)/shard_map/cond
  56.7 1.7 %copy-start.11 = (pred[8,9]{0,1:T(8,128)(4,1)S(1)}, pred[8,9]{0,1:T(8,128)(4,1)}, u32[]{:S(2)}) copy-start(pred[8,9]{0,1:T(8,128)(4,1)} %constant.46) | copy-start | bytes 220 | tf_op jit(solution)/shard_map/cond
  62.6 6.7 %copy-start.5 = (bf16[3,3,384,384]{3,2,1,0:T(8,128)(2,1)S(1)}, bf16[3,3,384,384]{3,2,1,0:T(8,128)(2,1)}, u32[]{:S(2)}) copy-start(bf16[3,3,384,384]{3,2,1,0:T(8,128)(2,1)} %param.22) | copy-start | bytes 7962628
  62.6 6.7 %copy-start.7 = (f32[384]{0:T(512)S(1)}, f32[384]{0:T(512)}, u32[]{:S(2)}) copy-start(f32[384]{0:T(512)} %param.23) | copy-start | bytes 4612
  63.1 2.9 %collective-permute-start.3 = (bf16[2,2,1,64,384]{4,1,3,2,0:T(2,128)(2,1)S(1)}, bf16[2,2,1,64,384]{4,1,3,2,0:T(2,128)(2,1)S(1)}, u32[]{:S(2)}, u32[]{:S(2)}) collective-permute-start(bf16[2,2,1,64,384]{4,1,3,2,0:T(2,128)(2,1)S(1)} %get-tuple-element.107), channel_id=1, source_target_pairs={{0,1},{2,3},{4,5},{6,7},{8,9},{10,11},{12,13},{14,15},{16,17},{18,... | collective-permute-start | bytes 589832 | tf_op jit(solution)/shard_map/ppermute | solution.py:20
  64.7 3.3 %collective-permute-start.4 = (bf16[2,2,1,64,384]{4,1,3,2,0:T(2,128)(2,1)S(1)}, bf16[2,2,1,64,384]{4,1,3,2,0:T(2,128)(2,1)S(1)}, u32[]{:S(2)}, u32[]{:S(2)}) collective-permute-start(bf16[2,2,1,64,384]{4,1,3,2,0:T(2,128)(2,1)S(1)} %get-tuple-element.108), channel_id=1, source_target_pairs={{1,0},{3,2},{5,4},{7,6},{9,8},{11,10},{13,12},{15,14},{17,16},{19,... | collective-permute-start | bytes 589832 | tf_op jit(solution)/shard_map/ppermute | solution.py:22
  72.9 1.6 %copy-start.8 = (pred[16,17]{0,1:T(8,128)(4,1)S(1)}, pred[16,17]{0,1:T(8,128)(4,1)}, u32[]{:S(2)}) copy-start(pred[16,17]{0,1:T(8,128)(4,1)} %constant.45) | copy-start | bytes 820 | tf_op jit(solution)/shard_map/cond
  83.1 1.8 %copy-start.6 = (bf16[3,3,384,384]{3,2,1,0:T(8,128)(2,1)S(1)}, bf16[3,3,384,384]{3,2,1,0:T(8,128)(2,1)}, u32[]{:S(2)}) copy-start(bf16[3,3,384,384]{3,2,1,0:T(8,128)(2,1)} %get-tuple-element.74) | copy-start | bytes 7962628 | tf_op jit(solution)/shard_map/cond
  83.1 1.7 %copy-start.9 = (pred[16,17]{0,1:T(8,128)(4,1)S(1)}, pred[16,17]{0,1:T(8,128)(4,1)}, u32[]{:S(2)}) copy-start(pred[16,17]{0,1:T(8,128)(4,1)} %constant.44) | copy-start | bytes 820 | tf_op jit(solution)/shard_map/cond
where the time goes:
time: 91.5 us; the launch traced here: 91.1 us
  waiting for transfers between devices  19.2 us (21%)
  local copies, waits for them, and re-layouts  18.8 us (21%)
  blocking collectives  18.1 us (20%)
  matrix products  15.1 us (17%)
  other arithmetic  10.4 us (11%)
  starting transfers between devices  6.85 us (7%)
  between operations  1.52 us (2%)
  loops' own time  1.11 us (1%)
    psum x1, blocking collectives, body(): total_first, total_second = lax.psum((first, second), ('tm', 'space'))  18.1 us
    ppermute x1, waiting for transfers between devices, from_behind(): lax.ppermute(value, axis, [(source, source + steps) for source in range(f...  15.2 us
    conv_general_dilated x2, matrix products, planar_section(): lax.conv_general_dilated(flat, conv2_weight, (1, 1), ((0, 0), (1, 1)), di...  8.39 us
    conv_general_dilated x2, matrix products, conv_volume(): lax.conv_general_dilated(stacked, kernel, (1, 1, 1), ((0, 0), (0, 0), (1,...  6.71 us
    ppermute x2, waiting for transfers between devices, extended(): lax.ppermute(head, axis, [((i + 1) % count, i) for i in range(ends)])  4.05 us
    another operation x6, local copies, waits for them, and re-layouts  3.8 us
    reshape x4, local copies, waits for them, and re-layouts, planar_section(): upsampled.reshape(count * frames_dev, 2 * rows_dev + 2, 2 * columns, chan...  3.51 us
    ppermute x2, starting transfers between devices, extended(): lax.ppermute(tail, axis, [(i, (i + 1) % count) for i in range(ends)])  2.92 us
  transfers between devices with their start and end apart: 5, of which 3 were waited for; matrix products, arithmetic and copies ran while one was open for 1% of the time, Pallas kernels for 0%

commit v1 on v0

v1 whole, which is shorter than its diff:
```python
import functools

import jax
import jax.numpy as jnp
from jax import lax
from jax.experimental import pallas as pl
from jax.experimental.pallas import tpu as pltpu
from jax.sharding import PartitionSpec as P

GROUPS = 32
EPSILON = 1e-05
MIB = 1 << 20

VMEM = pl.BlockSpec(memory_space=pltpu.VMEM)
SMEM = pl.BlockSpec(memory_space=pltpu.SMEM)
ANY = pl.BlockSpec(memory_space=pl.ANY)


def edge_rows(rows, count, place):
    if count == 2:
        return [jnp.where(place == 0, rows - 1, 0)]
    return [0, rows - 1]


def exchange(edges, axis):
    count = lax.axis_size(axis)
    if count == 2:
        other = lax.ppermute(edges[0], axis, [(0, 1), (1, 0)])
        return other, other
    first, last = edges
    above = lax.ppermute(last, axis, [(i, (i + 1) % count) for i in range(count)])
    below = lax.ppermute(first, axis, [((i + 1) % count, i) for i in range(count)])
    return above, below


def all_sum(value, axis):
    count = lax.axis_size(axis)
    if count & (count - 1):
        return lax.psum(value, axis)
    step = 1
    while step < count:
        value = value + lax.ppermute(value, axis, [(i, i ^ step) for i in range(count)])
        step *= 2
    return value


def stats_kernel(frames, count, scal, x, sums, *edges):
    clips, _, rows, columns, channels = x.shape
    parts = []
    for c in range(clips):
        first = jnp.zeros((columns, channels), jnp.float32)
        second = jnp.zeros((columns, channels), jnp.float32)
        for f in range(frames):
            keep = scal[0] + f < scal[2 + c]
            for r in range(rows):
                v = jnp.where(keep, x[c, f, r].astype(jnp.float32), 0.0)
                first = first + v
                second = second + v * v
        parts.append(jnp.sum(first, axis=0, keepdims=True))
        parts.append(jnp.sum(second, axis=0, keepdims=True))
    total = jnp.concatenate(parts, axis=0)
    high = total.astype(jnp.bfloat16)
    rest = total - high.astype(jnp.float32)
    middle = rest.astype(jnp.bfloat16)
    low = (rest - middle.astype(jnp.float32)).astype(jnp.bfloat16)
    width = channels // GROUPS
    group = lambda dim: jnp.floor(
        (lax.broadcasted_iota(jnp.int32, (channels, channels), dim).astype(jnp.float32) + 0.5)
        * (1.0 / width)
    )
    same = (group(0) == group(1)).astype(jnp.bfloat16)
    split = jnp.concatenate([high, middle, low], axis=0)
    summed = jnp.dot(split, same, preferred_element_type=jnp.float32)
    n = 2 * clips
    sums[...] = summed[:n] + summed[n : 2 * n] + summed[2 * n :]
    for e, row in zip(edges, edge_rows(rows, count, scal[1])):
        e[...] = x[:, :, pl.ds(row, 1)]


def shifted(value, step):
    size = value.shape[0]
    at = lax.broadcasted_iota(jnp.int32, value.shape, 0)
    rolled = pltpu.roll(value, step % size, 0)
    return jnp.where(at == (0 if step > 0 else size - 1), 0.0, rolled)


def put_three(dst, index, value, channels):
    dst[(*index, slice(None), slice(channels, 2 * channels))] = value.astype(jnp.bfloat16)
    dst[(*index, slice(None), slice(0, channels))] = shifted(value, 1).astype(jnp.bfloat16)
    dst[(*index, slice(None), slice(2 * channels, 3 * channels))] = shifted(value, -1).astype(jnp.bfloat16)


def block_kernel(
    count, per_count, scal, sums, gain, bias, bias3, own, own_top, own_bottom, past, past_top, past_bottom,
    weight, mid, *rest
):
    edges, (act, kern, sem) = rest[:-3], rest[-3:]
    clips, frames, rows, columns, channels = own.shape
    taps = weight.shape[0]
    span = 3 * channels
    copies = []
    for a in range(taps):
        copies.append(
            pltpu.make_async_copy(
                weight.at[taps - 1 - a], kern.at[:, pl.ds(a * channels, channels)], sem.at[a]
            )
        )
        copies[-1].start()
    place = scal[1]
    for c in range(clips):
        n = (scal[2 + c] * per_count).astype(jnp.float32)
        mean = sums[2 * c : 2 * c + 1, :] / n
        variance = sums[2 * c + 1 : 2 * c + 2, :] / n - mean * mean
        scale = lax.rsqrt(variance + EPSILON) * gain[...]
        offset = bias[...] - mean * scale
        for f in range(2 + frames):
            if f < 2:
                body, top, bottom, at = past, past_top, past_bottom, f + frames - 2
            else:
                body, top, bottom, at = own, own_top, own_bottom, f - 2
            moment = scal[0] + f - 2
            live = jnp.logical_and(moment >= 0, moment < scal[2 + c])
            for r in range(rows + 2):
                if r == 0:
                    raw, keep = top[c, at, 0], jnp.logical_and(live, place > 0)
                elif r == rows + 1:
                    raw, keep = bottom[c, at, 0], jnp.logical_and(live, place < count - 1)
                else:
                    raw, keep = body[c, at, r - 1], live
                v = raw.astype(jnp.float32) * scale + offset
                v = v / (1.0 + jnp.exp(-v))
                put_three(act, (f, r, c), jnp.where(keep, v, 0.0), channels)
    size = rows * clips * columns

    def left(f):
        return jnp.concatenate(
            [act[f, b : b + rows].reshape(size, span) for b in range(3)], axis=1
        )

    def part(f, low, high):
        return jnp.dot(
            left(f), kern[:, low * channels : high * channels], preferred_element_type=jnp.float32
        )

    for copy in copies:
        copy.wait()
    assert frames == 2 and taps == 3
    two = part(2, 0, 2)
    out = [two[:, :channels], two[:, channels:] + part(3, 0, 1)]
    one = part(1, 1, 3)
    out = [out[0] + one[:, :channels] + part(0, 2, 3), out[1] + one[:, channels:]]
    for f in range(frames):
        for c in range(clips):
            live = scal[0] + f < scal[2 + c]
            for r in range(rows):
                start = (r * clips + c) * columns
                value = own[c, f, r].astype(jnp.float32) + out[f][start : start + columns] + bias3[...]
                mid[r, f, c] = jnp.where(live, value, 0.0).astype(jnp.bfloat16)
    for e, row in zip(edges, edge_rows(rows, count, place)):
        e[...] = mid[pl.ds(row, 1)]


def fold_kernel(weight, out):
    taps = ((((0,), (1, 2)), ((0, 1), (2,))))
    for p in range(2):
        for r in range(2):
            by_column = []
            for e in range(3):
                total = None
                for b in taps[p][r]:
                    v = weight[b, e].astype(jnp.float32)
                    total = v if total is None else total + v
                by_column.append(total)
            for q in range(2):
                for s in range(2):
                    total = None
                    for e in taps[q][s]:
                        total = by_column[e] if total is None else total + by_column[e]
                    out[p, q, r, s] = total.astype(jnp.bfloat16)


def planar_kernel(count, scal, mid, top, bottom, kern, bias2, out, wide, lines):
    rows, frames, clips, columns, channels = mid.shape
    place = scal[1]
    for r in range(rows + 2):
        for f in range(frames):
            for c in range(clips):
                if r == 0:
                    v = jnp.where(place > 0, top[0, f, c].astype(jnp.float32), 0.0)
                elif r == rows + 1:
                    v = jnp.where(place < count - 1, bottom[0, f, c].astype(jnp.float32), 0.0)
                else:
                    v = mid[r - 1, f, c].astype(jnp.float32)
                put_three(wide, (r, f, c), v, channels)
    size = rows * frames * clips * columns
    for p in range(2):
        for q in range(2):
            low = q * channels
            left = jnp.concatenate(
                [
                    wide[p + r : p + r + rows, :, :, :, low : low + 2 * channels].reshape(size, 2 * channels)
                    for r in range(2)
                ],
                axis=1,
            )
            part = jnp.dot(
                left, kern[p, q].reshape(4 * channels, channels), preferred_element_type=jnp.float32
            )
            for i in range(rows):
                for f in range(frames):
                    for c in range(clips):
                        start = ((i * frames + f) * clips + c) * columns
                        for k in range(channels // 128):
                            lines[k, (i * frames + f) * clips + c, pl.ds(q, columns, stride=2), :] = part[
                                start : start + columns, k * 128 : k * 128 + 128
                            ]
        for i in range(rows):
            for f in range(frames):
                for c in range(clips):
                    live = scal[0] + f < scal[2 + c]
                    for k in range(channels // 128):
                        lanes = slice(k * 128, k * 128 + 128)
                        value = lines[k, (i * frames + f) * clips + c] + bias2[:, lanes]
                        out[c, f, 2 * i + p, :, lanes] = jnp.where(live, value, 0.0).astype(jnp.bfloat16)


def body(
    latents, frame_counts, norm_gain, norm_bias, conv3_weight, conv3_bias, conv2_weight, conv2_bias
):
    clips, frames, rows, columns, channels = latents.shape
    count = lax.axis_size("space")
    behind = lax.axis_size("tm")
    per_count = rows * count * columns * (channels // GROUPS)
    scal = jnp.concatenate(
        [
            jnp.stack([lax.axis_index("tm") * frames, lax.axis_index("space")]).astype(jnp.int32),
            frame_counts,
        ]
    )
    params = lambda mib: pltpu.CompilerParams(vmem_limit_bytes=mib * MIB)
    n_edges = 1 if count == 2 else 2
    f32, bf16 = jnp.float32, jnp.bfloat16
    shape = jax.ShapeDtypeStruct
    cost = lambda flops, size: pl.CostEstimate(flops=int(flops), bytes_accessed=int(size), transcendentals=0)

    past = lax.ppermute(latents, "tm", [(i, (i + 1) % behind) for i in range(behind)])
    stats = pl.pallas_call(
        functools.partial(stats_kernel, frames, count),
        out_shape=[shape((2 * clips, channels), f32)]
        + [shape((clips, frames, 1, columns, channels), bf16)] * n_edges,
        in_specs=[SMEM, VMEM],
        out_specs=[VMEM] * (1 + n_edges),
        compiler_params=params(8),
        name="stats",
    )(scal, latents)
    sums = all_sum(all_sum(stats[0], "space"), "tm")
    own_top, own_bottom = exchange(stats[1:], "space")
    place = lax.axis_index("space")
    past_edges = [
        lax.dynamic_slice_in_dim(past, row, 1, axis=2) for row in edge_rows(rows, count, place)
    ]
    past_top, past_bottom = exchange(past_edges, "space")

    folded = pl.pallas_call(
        fold_kernel,
        out_shape=shape((2, 2, 2, 2, channels, channels), bf16),
        in_specs=[VMEM],
        out_specs=VMEM,
        compiler_params=params(16),
        cost_estimate=cost(4e7, 8e6),
        name="fold",
    )(conv2_weight)

    taps = conv3_weight.shape[0]
    line = lambda v: v.reshape(1, channels)
    block = pl.pallas_call(
        functools.partial(block_kernel, count, per_count),
        out_shape=[shape((rows, frames, clips, columns, channels), bf16)]
        + [shape((1, frames, clips, columns, channels), bf16)] * n_edges,
        in_specs=[SMEM] + [VMEM] * 10 + [ANY],
        out_specs=[VMEM] * (1 + n_edges),
        scratch_shapes=[
            pltpu.VMEM((frames + 2, rows + 2, clips, columns, 3 * channels), bf16),
            pltpu.VMEM((9 * channels, taps * channels), bf16),
            pltpu.SemaphoreType.DMA((taps,)),
        ],
        compiler_params=params(40),
        cost_estimate=cost(4e9, 1e7),
        name="block",
    )(
        scal, sums, line(norm_gain), line(norm_bias), line(conv3_bias), latents, own_top, own_bottom,
        past, past_top, past_bottom, conv3_weight.reshape(taps, 9 * channels, channels),
    )
    mid = block[0]
    mid_top, mid_bottom = exchange(block[1:], "space")
    return pl.pallas_call(
        functools.partial(planar_kernel, count),
        out_shape=shape((clips, frames, 2 * rows, 2 * columns, channels), bf16),
        in_specs=[SMEM] + [VMEM] * 5,
        out_specs=VMEM,
        scratch_shapes=[
            pltpu.VMEM((rows + 2, frames, clips, columns, 3 * channels), bf16),
            pltpu.VMEM((channels // 128, rows * frames * clips, 2 * columns, 128), f32),
        ],
        compiler_params=params(40),
        cost_estimate=cost(3e9, 8e6),
        name="planar",
    )(scal, mid, mid_top, mid_bottom, folded, line(conv2_bias))


def solution(mesh):
    placed = (P("clip", "tm", "space", None, None), P("clip"), P(), P(), P(), P(), P(), P())
    return jax.shard_map(
        body,
        mesh=mesh,
        in_specs=placed,
        out_specs=P("clip", "tm", "space", None, None),
        check_vma=False,
    )
```

time: 91.5 us -> 43.6 us (0.48)
  blocking collectives: 18.1 us -> 0 us
  Pallas kernels: 0 us -> 15.3 us
  matrix products: 15.1 us -> 0 us
  local copies, waits for them, and re-layouts: 18.8 us -> 7.33 us
  other arithmetic: 10.4 us -> 0.74 us
  waiting for transfers between devices: 19.2 us -> 15.4 us
  starting transfers between devices: 6.85 us -> 4.43 us
  between operations: 1.52 us -> 0.1 us
  loops' own time: 1.11 us -> 0 us
    psum x1 -> x0, blocking collectives: 18.1 us -> none  [body(): total_first, total_second = lax.psum((first, second), ('tm', 'space'))]
    pallas_call x0 -> x4, Pallas kernels: none -> 15.3 us  [the longest x1 8.12 us: body(): pl.pallas_call(functools.partial(block_kernel, count, per_count), out_sha...]
    conv_general_dilated x4 -> x0, matrix products: 15.1 us -> none  [the longest x2 8.39 us: planar_section(): lax.conv_general_dilated(flat, conv2_weight, (1, 1), ((0, 0), (1, 1)), di...]
    unnamed x11 -> x10, local copies, waits for them, and re-layouts: 0.17 us -> 5.26 us
    another operation x6 -> x0, local copies, waits for them, and re-layouts: 3.8 us -> none
    ppermute x5 -> x7, waiting for transfers between devices: 19.2 us -> 15.4 us  [the longest x1 8.73 us: body(): lax.ppermute(latents, 'tm', [(i, (i + 1) % behind) for i in range(behind)])]
    convert_element_type x5 -> x0, other arithmetic: 3.29 us -> none  [the longest x1 1.33 us: body(): activated = (jax.nn.silu(shifted) * broad_mask).astype(jnp.bfloat16)]
    cond x18 -> x0, local copies, waits for them, and re-layouts: 3.2 us -> none
  transfers between devices with their start and end apart: 5 -> 7, of which waited for: 3 -> 5; matrix products, arithmetic and copies ran while one was open for 1% -> 6% of each run, Pallas kernels for 0% -> 4%
where the time goes in v1:
time: 43.6 us; the launch traced here: 43.3 us
  waiting for transfers between devices  15.4 us (35%)
  Pallas kernels  15.3 us (35%)
  local copies, waits for them, and re-layouts  7.33 us (17%)
  starting transfers between devices  4.43 us (10%)
  other arithmetic  0.74 us (2%)
    ppermute x1, waiting for transfers between devices, body(): lax.ppermute(latents, 'tm', [(i, (i + 1) % behind) for i in range(behind)])  8.73 us
    pallas_call x1, Pallas kernels, body(): pl.pallas_call(functools.partial(block_kernel, count, per_count), out_sha...  8.12 us
    ppermute x3, waiting for transfers between devices, all_sum(): lax.ppermute(value, axis, [(i, i ^ step) for i in range(count)])  6.31 us
    pallas_call x1, Pallas kernels, body(): pl.pallas_call(functools.partial(planar_kernel, count), out_shape=shape((...  5.28 us
    unnamed x10, local copies, waits for them, and re-layouts  5.26 us
    ppermute x1, starting transfers between devices, body(): lax.ppermute(latents, 'tm', [(i, (i + 1) % behind) for i in range(behind)])  3.05 us
    reshape x4, local copies, waits for them, and re-layouts, body(): line = lambda v: v.reshape(1, channels)  2.05 us
    ppermute x3, starting transfers between devices, all_sum(): lax.ppermute(value, axis, [(i, i ^ step) for i in range(count)])  1.23 us
  transfers between devices with their start and end apart: 7, of which 5 were waited for; matrix products, arithmetic and copies ran while one was open for 6% of the time, Pallas kernels for 4%

profile of v1, /device:TPU:0, one launch (start us, length us, event | category | flops | bytes accessed | tf_op | source)
XLA Modules:
  0.0 43.3 jit_solution(8300640869086658257)
XLA Ops:
  0.0 3.1 %collective-permute-start.4 = (bf16[2,2,2,64,384]{4,3,2,1,0:T(8,128)(2,1)}, bf16[2,2,2,64,384]{4,3,2,1,0:T(8,128)(2,1)S(1)}, u32[]{:S(2)}, u32[]{:S(2)}) collective-permute-start(bf16[2,2,2,64,384]{4,3,2,1,0:T(8,128)(2,1)} %own.1), channel_id=1, source_target_pairs={{0,2},{2,4},{4,6},{6,0},{1,3},{3,5},{5,7},{7,1},{8,10},{10,12},{12... | collective-permute-start | bytes 1179656 | tf_op jit(solution)/shard_map/ppermute | solution.py:246
  3.1 0.7 %pad_add_fusion.scal = s32[4]{0:T(128)S(1)} fusion(s32[2]{0:T(128)} %param.9, s32[1]{0:T(128)} %bitcast.1, s32[1]{0:T(128)} %bitcast), kind=kLoop, calls=%fused_computation | loop fusion | flops 8 | bytes 32 | tf_op jit(solution)/shard_map/concatenate | solution.py:234
  3.8 0.0 copy-start.1
  3.8 1.0 %copy-done.1 = bf16[2,2,2,64,384]{4,3,2,1,0:T(8,128)(2,1)S(1)} copy-done((bf16[2,2,2,64,384]{4,3,2,1,0:T(8,128)(2,1)S(1)}, bf16[2,2,2,64,384]{4,3,2,1,0:T(8,128)(2,1)}, u32[]{:S(2)}) %copy-start.1) | copy-done | bytes 393240
  4.8 0.9 %stats.1 = (f32[4,384]{1,0:T(4,128)S(1)}, bf16[2,2,1,64,384]{4,3,2,1,0:T(8,128)(2,1)S(1)}) custom-call(s32[4]{0:T(128)S(1)} %pad_add_fusion.scal, bf16[2,2,2,64,384]{4,3,2,1,0:T(8,128)(2,1)S(1)} %copy-done.1), custom_call_target="tpu_custom_call" | custom-call | tf_op jit(solution)/shard_map/stats/pallas_call | solution.py:247
  5.7 0.0 collective-permute-start.3
  5.7 8.7 %collective-permute-done.4.past = bf16[2,2,2,64,384]{4,3,2,1,0:T(8,128)(2,1)S(1)} collective-permute-done((bf16[2,2,2,64,384]{4,3,2,1,0:T(8,128)(2,1)}, bf16[2,2,2,64,384]{4,3,2,1,0:T(8,128)(2,1)S(1)}, u32[]{:S(2)}, u32[]{:S(2)}) %collective-permute-start.4) | collective-permute-done | bytes 393248 | tf_op jit(solution)/shard_map/ppermute | solution.py:246
  14.4 0.1 collective-permute-start.5
  14.5 0.5 %collective-permute-start = (f32[4,384]{1,0:T(4,128)S(1)}, f32[4,384]{1,0:T(4,128)S(1)}, u32[]{:S(2)}, u32[]{:S(2)}) collective-permute-start(f32[4,384]{1,0:T(4,128)S(1)} %get-tuple-element.9), channel_id=1, source_target_pairs={{0,1},{1,0},{2,3},{3,2},{4,5},{5,4},{6,7},{7,6},{8,9},{9,8},{10,11... | collective-permute-start | bytes 18440 | tf_op jit(solution)/shard_map/ppermute | solution.py:42
  15.0 0.9 %collective-permute-done = f32[4,384]{1,0:T(4,128)S(1)} collective-permute-done((f32[4,384]{1,0:T(4,128)S(1)}, f32[4,384]{1,0:T(4,128)S(1)}, u32[]{:S(2)}, u32[]{:S(2)}) %collective-permute-start) | collective-permute-done | bytes 6176 | tf_op jit(solution)/shard_map/ppermute | solution.py:42
  15.9 0.0 collective-permute-start.1
  15.9 3.6 %collective-permute-done.1 = f32[4,384]{1,0:T(4,128)S(1)} collective-permute-done((f32[4,384]{1,0:T(4,128)S(1)}, f32[4,384]{1,0:T(4,128)S(1)}, u32[]{:S(2)}, u32[]{:S(2)}) %collective-permute-start.1) | collective-permute-done | bytes 6176 | tf_op jit(solution)/shard_map/ppermute | solution.py:42
  19.6 0.7 %collective-permute-start.2 = (f32[4,384]{1,0:T(4,128)S(1)}, f32[4,384]{1,0:T(4,128)S(1)}, u32[]{:S(2)}, u32[]{:S(2)}) collective-permute-start(f32[4,384]{1,0:T(4,128)S(1)} %add.11), channel_id=1, source_target_pairs={{0,4},{2,6},{4,0},{6,2},{1,5},{3,7},{5,1},{7,3},{8,12},{10,14},{12... | collective-permute-start | bytes 18440 | tf_op jit(solution)/shard_map/ppermute | solution.py:42
  20.3 0.7 %reshape.15.gain = f32[1,384]{1,0:T(1,128)S(1)} reshape(f32[384]{0:T(512)} %param.10) | data formatting | bytes 3072 | tf_op jit(solution)/shard_map/reshape | solution.py:275
  21.0 0.7 %reshape.16.bias = f32[1,384]{1,0:T(1,128)S(1)} reshape(f32[384]{0:T(512)} %param.11) | data formatting | bytes 3072 | tf_op jit(solution)/shard_map/reshape | solution.py:275
  21.7 0.7 %reshape.17.bias3 = f32[1,384]{1,0:T(1,128)S(1)} reshape(f32[384]{0:T(512)} %param.13) | data formatting | bytes 3072 | tf_op jit(solution)/shard_map/reshape | solution.py:275
  22.4 1.7 %collective-permute-done.2 = f32[4,384]{1,0:T(4,128)S(1)} collective-permute-done((f32[4,384]{1,0:T(4,128)S(1)}, f32[4,384]{1,0:T(4,128)S(1)}, u32[]{:S(2)}, u32[]{:S(2)}) %collective-permute-start.2) | collective-permute-done | bytes 6176 | tf_op jit(solution)/shard_map/ppermute | solution.py:42
  24.1 0.0 collective-permute-done.3.own_top.own_bottom
  24.1 0.0 collective-permute-done.5.past_top.past_bottom
  24.1 0.0 copy-start.2
  24.1 1.0 %copy-done.2 = bf16[2,2,2,64,384]{4,3,2,1,0:T(8,128)(2,1)S(1)} copy-done((bf16[2,2,2,64,384]{4,3,2,1,0:T(8,128)(2,1)S(1)}, bf16[2,2,2,64,384]{4,3,2,1,0:T(8,128)(2,1)}, u32[]{:S(2)}) %copy-start.2) | copy-done | bytes 393240
  25.1 0.0 copy-start.3
  25.1 3.3 %copy-done.3 = bf16[3,3,3,384,384]{4,3,2,1,0:T(8,128)(2,1)S(1)} copy-done((bf16[3,3,3,384,384]{4,3,2,1,0:T(8,128)(2,1)S(1)}, bf16[3,3,3,384,384]{4,3,2,1,0:T(8,128)(2,1)}, u32[]{:S(2)}) %copy-start.3) | copy-done | bytes 7962648
  28.4 0.0 copy-start.4
  28.4 0.0 copy-start
  28.4 8.1 %block.1 = (bf16[2,2,2,64,384]{4,3,2,1,0:T(8,128)(2,1)S(1)}, bf16[1,2,2,64,384]{4,3,2,1,0:T(8,128)(2,1)S(1)}) custom-call(s32[4]{0:T(128)S(1)} %pad_add_fusion.scal, f32[4,384]{1,0:T(4,128)S(1)} %add.12.sums, f32[1,384]{1,0:T(1,128)S(1)} %reshape.15.gain, f32[1,384]{1,0:T(1,128)S(1)} %reshape.16.bias, f32[1,384]{1,0:T(1,128)S(1)} %reshape.17.bias3, ...), custom_call_target="tpu_custom_call" | custom-call | flops 4000000000 | bytes 10000000 | tf_op jit(solution)/shard_map/block/pallas_call | solution.py:276
  36.5 0.1 collective-permute-start.6
  36.6 0.0 copy-done.4
  36.6 0.0 copy-done
  36.6 1.0 %fold.1.kern = bf16[2,2,2,2,384,384]{5,4,3,2,1,0:T(8,128)(2,1)S(1)} custom-call(bf16[3,3,384,384]{3,2,1,0:T(8,128)(2,1)S(1)} %copy-done), custom_call_target="tpu_custom_call" | custom-call | flops 40000000 | bytes 8000000 | tf_op jit(solution)/shard_map/fold/pallas_call | solution.py:264
  37.6 0.4 collective-permute-done.6.top.bottom
  38.0 5.3 %planar.1 = bf16[2,2,4,128,384]{4,3,2,1,0:T(8,128)(2,1)} custom-call(s32[4]{0:T(128)S(1)} %pad_add_fusion.scal, bf16[2,2,2,64,384]{4,3,2,1,0:T(8,128)(2,1)S(1)} %get-tuple-element.11.mid, bf16[1,2,2,64,384]{4,3,2,1,0:T(8,128)(2,1)S(1)} %collective-permute-done.6.top.bottom, bf16[1,2,2,64,384]{4,3,2,1,0:T(8,128)(2,1)S(1)} %collective-permute-done.6.top.bottom, ...), custom_call_target="tpu_custom_call" | custom-call | flops 3000000000 | bytes 8000000 | tf_op jit(solution)/shard_map/planar/pallas_call | solution.py:296
  (5 shorter events, 0.0 us)
Async XLA Ops:
  0.0 14.4 %collective-permute-start.4 = (bf16[2,2,2,64,384]{4,3,2,1,0:T(8,128)(2,1)}, bf16[2,2,2,64,384]{4,3,2,1,0:T(8,128)(2,1)S(1)}, u32[]{:S(2)}, u32[]{:S(2)}) collective-permute-start(bf16[2,2,2,64,384]{4,3,2,1,0:T(8,128)(2,1)} %own.1), channel_id=1, source_target_pairs={{0,2},{2,4},{4,6},{6,0},{1,3},{3,5},{5,7},{7,1},{8,10},{10,12},{12... | collective-permute-start | bytes 1179656 | tf_op jit(solution)/shard_map/ppermute | solution.py:246
  3.8 1.0 %copy-start.1 = (bf16[2,2,2,64,384]{4,3,2,1,0:T(8,128)(2,1)S(1)}, bf16[2,2,2,64,384]{4,3,2,1,0:T(8,128)(2,1)}, u32[]{:S(2)}) copy-start(bf16[2,2,2,64,384]{4,3,2,1,0:T(8,128)(2,1)} %own.1) | copy-start | bytes 1179652
  5.7 18.5 %collective-permute-start.3 = (bf16[2,2,1,64,384]{4,3,2,1,0:T(8,128)(2,1)S(1)}, bf16[2,2,1,64,384]{4,3,2,1,0:T(8,128)(2,1)S(1)}, u32[]{:S(2)}, u32[]{:S(2)}) collective-permute-start(bf16[2,2,1,64,384]{4,3,2,1,0:T(8,128)(2,1)S(1)} %get-tuple-element.10), channel_id=1, source_target_pairs={{0,1},{1,0},{2,3},{3,2},{4,5},{5,4},{6,7},{7,6},{8,9},{9,8},{10,11... | collective-permute-start | bytes 589832 | tf_op jit(solution)/shard_map/ppermute | solution.py:28
  14.4 9.7 %collective-permute-start.5 = (bf16[2,2,1,64,384]{4,3,2,1,0:T(8,128)(2,1)S(1)}, bf16[2,2,1,64,384]{4,3,2,1,0:T(8,128)(2,1)S(1)}, u32[]{:S(2)}, u32[]{:S(2)}) collective-permute-start(bf16[2,2,1,64,384]{4,3,2,1,0:T(8,128)(2,1)S(1)} %constant_dynamic-slice_fusion), channel_id=1, source_target_pairs={{0,1},{1,0},{2,3},{3,2},{4,5},{5,4},{6,7},{7,6},{8,9},{9,8},{10,11... | collective-permute-start | bytes 589832 | tf_op jit(solution)/shard_map/ppermute | solution.py:28
  14.5 1.4 %collective-permute-start = (f32[4,384]{1,0:T(4,128)S(1)}, f32[4,384]{1,0:T(4,128)S(1)}, u32[]{:S(2)}, u32[]{:S(2)}) collective-permute-start(f32[4,384]{1,0:T(4,128)S(1)} %get-tuple-element.9), channel_id=1, source_target_pairs={{0,1},{1,0},{2,3},{3,2},{4,5},{5,4},{6,7},{7,6},{8,9},{9,8},{10,11... | collective-permute-start | bytes 18440 | tf_op jit(solution)/shard_map/ppermute | solution.py:42
  15.9 3.6 %collective-permute-start.1 = (f32[4,384]{1,0:T(4,128)S(1)}, f32[4,384]{1,0:T(4,128)S(1)}, u32[]{:S(2)}, u32[]{:S(2)}) collective-permute-start(f32[4,384]{1,0:T(4,128)S(1)} %add.10), channel_id=1, source_target_pairs={{0,2},{2,0},{4,6},{6,4},{1,3},{3,1},{5,7},{7,5},{8,10},{10,8},{12,... | collective-permute-start | bytes 18440 | tf_op jit(solution)/shard_map/ppermute | solution.py:42
  19.6 4.5 %collective-permute-start.2 = (f32[4,384]{1,0:T(4,128)S(1)}, f32[4,384]{1,0:T(4,128)S(1)}, u32[]{:S(2)}, u32[]{:S(2)}) collective-permute-start(f32[4,384]{1,0:T(4,128)S(1)} %add.11), channel_id=1, source_target_pairs={{0,4},{2,6},{4,0},{6,2},{1,5},{3,7},{5,1},{7,3},{8,12},{10,14},{12... | collective-permute-start | bytes 18440 | tf_op jit(solution)/shard_map/ppermute | solution.py:42
  24.1 1.0 %copy-start.2 = (bf16[2,2,2,64,384]{4,3,2,1,0:T(8,128)(2,1)S(1)}, bf16[2,2,2,64,384]{4,3,2,1,0:T(8,128)(2,1)}, u32[]{:S(2)}) copy-start(bf16[2,2,2,64,384]{4,3,2,1,0:T(8,128)(2,1)} %own.1) | copy-start | bytes 1179652
  25.1 3.3 %copy-start.3 = (bf16[3,3,3,384,384]{4,3,2,1,0:T(8,128)(2,1)S(1)}, bf16[3,3,3,384,384]{4,3,2,1,0:T(8,128)(2,1)}, u32[]{:S(2)}) copy-start(bf16[3,3,3,384,384]{4,3,2,1,0:T(8,128)(2,1)} %param.12) | copy-start | bytes 23887876
  28.4 8.2 %copy-start.4 = (f32[384]{0:T(512)S(1)}, f32[384]{0:T(512)}, u32[]{:S(2)}) copy-start(f32[384]{0:T(512)} %param.15) | copy-start | bytes 4612
  28.4 8.2 %copy-start = (bf16[3,3,384,384]{3,2,1,0:T(8,128)(2,1)S(1)}, bf16[3,3,384,384]{3,2,1,0:T(8,128)(2,1)}, u32[]{:S(2)}) copy-start(bf16[3,3,384,384]{3,2,1,0:T(8,128)(2,1)} %weight.1) | copy-start | bytes 7962628
  36.5 1.5 %collective-permute-start.6 = (bf16[1,2,2,64,384]{4,3,2,1,0:T(8,128)(2,1)S(1)}, bf16[1,2,2,64,384]{4,3,2,1,0:T(8,128)(2,1)S(1)}, u32[]{:S(2)}, u32[]{:S(2)}) collective-permute-start(bf16[1,2,2,64,384]{4,3,2,1,0:T(8,128)(2,1)S(1)} %get-tuple-element.12), channel_id=1, source_target_pairs={{0,1},{1,0},{2,3},{3,2},{4,5},{5,4},{6,7},{7,6},{8,9},{9,8},{10,11... | collective-permute-start | bytes 589832 | tf_op jit(solution)/shard_map/ppermute | solution.py:28

commit v2 on v0

v2 whole, which is shorter than its diff:
```python
import functools

import jax
import jax.numpy as jnp
from jax import lax
from jax.experimental import pallas as pl
from jax.experimental.pallas import tpu as pltpu
from jax.sharding import PartitionSpec as P

GROUPS = 32
EPSILON = 1e-05
MIB = 1 << 20
LANES = 128

VMEM = pl.BlockSpec(memory_space=pltpu.VMEM)
SMEM = pl.BlockSpec(memory_space=pltpu.SMEM)
HBM = pl.BlockSpec(memory_space=pltpu.HBM)
f32, bf16 = jnp.float32, jnp.bfloat16


def edge_rows(rows, count):
    if count == 2:
        return [jnp.where(lax.axis_index("space") == 0, rows - 1, 0)]
    return [0, rows - 1]


def exchange(edges, axis):
    count = lax.axis_size(axis)
    if count == 2:
        other = lax.ppermute(edges[0], axis, [(0, 1), (1, 0)])
        return other, other
    first, last = edges
    above = lax.ppermute(last, axis, [(i, (i + 1) % count) for i in range(count)])
    below = lax.ppermute(first, axis, [((i + 1) % count, i) for i in range(count)])
    return above, below


def all_sum(value, axis):
    count = lax.axis_size(axis)
    if count & (count - 1):
        return lax.psum(value, axis)
    step = 1
    while step < count:
        value = value + lax.ppermute(value, axis, [(i, i ^ step) for i in range(count)])
        step *= 2
    return value


def shifted(value, step):
    size = value.shape[0]
    at = lax.broadcasted_iota(jnp.int32, value.shape, 0)
    rolled = pltpu.roll(value, step % size, 0)
    return jnp.where(at == (0 if step > 0 else size - 1), 0.0, rolled)


def stats_kernel(count, counts, x, sums, *rest):
    clips, frames, rows, columns, channels = x.shape
    own, edges, sem = rest[:clips], rest[clips:-1], rest[-1]
    copies = []
    for c in range(clips):
        copies.append([])
        for f in range(frames):
            copies[c].append(pltpu.make_async_copy(x.at[c, f], own[c].at[f], sem.at[c, f]))
            copies[c][f].start()
    width = channels // GROUPS
    group = lambda dim: jnp.floor(
        (lax.broadcasted_iota(jnp.int32, (channels, channels), dim).astype(f32) + 0.5) * (1.0 / width)
    )
    same = (group(0) == group(1)).astype(bf16)
    start = lax.axis_index("tm") * frames
    parts = []
    for c in range(clips):
        first = jnp.zeros((columns, channels), f32)
        second = jnp.zeros((columns, channels), f32)
        for f in range(frames):
            copies[c][f].wait()
            keep = start + f < counts[c]
            for r in range(rows):
                v = jnp.where(keep, own[c][f, r].astype(f32), 0.0)
                first = first + v
                second = second + v * v
        parts.append(jnp.sum(first, axis=0, keepdims=True))
        parts.append(jnp.sum(second, axis=0, keepdims=True))
    total = jnp.concatenate(parts, axis=0)
    high = total.astype(bf16)
    left = total - high.astype(f32)
    middle = left.astype(bf16)
    low = (left - middle.astype(f32)).astype(bf16)
    split = jnp.concatenate([high, middle, low], axis=0)
    summed = jnp.dot(split, same, preferred_element_type=f32)
    n = 2 * clips
    sums[...] = summed[:n] + summed[n : 2 * n] + summed[2 * n :]
    for e, row in zip(edges, edge_rows(rows, count)):
        for c in range(clips):
            e[c] = own[c][:, pl.ds(row, 1)]


def activate(act, index, raw, keep, scale, offset):
    v = raw.astype(f32) * scale + offset
    v = v / (1.0 + jnp.exp(-v))
    act[index] = jnp.where(keep, v, 0.0).astype(bf16)


def keep_row(r, rows, count, live):
    place = lax.axis_index("space")
    if r == 0:
        return jnp.logical_and(live, place > 0)
    if r == rows + 1:
        return jnp.logical_and(live, place < count - 1)
    return live


def patch(act, f, rows):
    channels = act.shape[-1]
    return jnp.concatenate(
        [act[f, b : b + rows].reshape(-1, channels) for b in range(3)], axis=1
    )


def own_kernel(
    count, per_count, counts, sums, gain, bias, *rest
):
    clips = counts.shape[0]
    own, (top, bottom, weight), (acc, norm, past_kern, act, kern, sem) = rest[:clips], rest[clips : clips + 3], rest[clips + 3 :]
    frames, rows, columns, channels = own[0].shape
    copies = {}
    for a in (2, 1, 0):
        dst = kern if a == 2 else past_kern.at[pl.ds(3 * a, 3)]
        for e in range(3):
            copy = pltpu.make_async_copy(
                weight.at[a, :, e], dst.at[:, :, pl.ds(e * channels, channels)], sem.at[a, e]
            )
            copy.start()
            copies.setdefault(a, []).append(copy)
    start = lax.axis_index("tm") * frames
    for c in range(clips):
        n = (counts[c] * per_count).astype(f32)
        mean = sums[2 * c : 2 * c + 1, :] / n
        variance = sums[2 * c + 1 : 2 * c + 2, :] / n - mean * mean
        scale = lax.rsqrt(variance + EPSILON) * gain[...].reshape(1, channels)
        offset = bias[...].reshape(1, channels) - mean * scale
        norm[c, 0:1] = scale
        norm[c, 1:2] = offset
    for f in range(frames):
        for c in range(clips):
            scale, offset = norm[c, 0:1], norm[c, 1:2]
            live = start + f < counts[c]
            for r in range(rows + 2):
                raw = top[c, f, 0] if r == 0 else bottom[c, f, 0] if r == rows + 1 else own[c][f, r - 1]
                activate(act, (f, r, c), raw, keep_row(r, rows, count, live), scale, offset)
    span = 3 * channels

    def store(t, part):
        for r in range(rows):
            for c in range(clips):
                low = (r * clips + c) * columns
                block = part[low : low + columns]
                acc[t, c, r] = (
                    shifted(block[:, :channels], 1)
                    + block[:, channels : 2 * channels]
                    + shifted(block[:, 2 * channels :], -1)
                )

    assert frames == 2
    for copy in copies[2]:
        copy.wait()
    store(0, jnp.dot(patch(act, 0, rows), kern[...].reshape(span, span), preferred_element_type=f32))
    for copy in copies[1]:
        copy.wait()
    both = jnp.concatenate([past_kern[3:6].reshape(span, span), kern[...].reshape(span, span)], axis=0)
    store(
        1,
        jnp.dot(
            jnp.concatenate([patch(act, 0, rows), patch(act, 1, rows)], axis=1),
            both,
            preferred_element_type=f32,
        ),
    )
    for copy in copies[0]:
        copy.wait()


def past_kernel(
    count, clip, counts, norm, bias3, acc, past_kern, own, past, top, bottom, mid, *rest
):
    edges, act = rest[:-1], rest[-1]
    frames, rows, columns, channels = own.shape
    span = 3 * channels
    start = lax.axis_index("tm") * frames
    scale, offset = norm[clip, 0:1], norm[clip, 1:2]
    for g in range(2):
        at = frames - 2 + g
        moment = start - 2 + g
        live = jnp.logical_and(moment >= 0, moment < counts[clip])
        for r in range(rows + 2):
            raw = top[at, 0] if r == 0 else bottom[at, 0] if r == rows + 1 else past[at, r - 1]
            activate(act, (g, r), raw, keep_row(r, rows, count, live), scale, offset)

    def store(t, part):
        live = start + t < counts[clip]
        for r in range(rows):
            block = part[r * columns : (r + 1) * columns]
            value = (
                shifted(block[:, :channels], 1)
                + block[:, channels : 2 * channels]
                + shifted(block[:, 2 * channels :], -1)
            )
            value = value + acc[t, clip, r] + own[t, r].astype(f32) + bias3[...].reshape(1, channels)
            mid[r, t] = jnp.where(live, value, 0.0).astype(bf16)

    older, newer = patch(act, 0, rows), patch(act, 1, rows)
    store(1, jnp.dot(newer, past_kern[0:3].reshape(span, span), preferred_element_type=f32))
    store(
        0,
        jnp.dot(
            jnp.concatenate([older, newer], axis=1),
            past_kern[...].reshape(2 * span, span),
            preferred_element_type=f32,
        ),
    )
    for e, row in zip(edges, edge_rows(rows, count)):
        e[...] = mid[pl.ds(row, 1)]


PHASES = (((0,), (1, 2)), ((0, 1), (2,)))


def fold_kernel(weight, out):
    channels = weight.shape[-1]
    for p in range(2):
        for r in range(2):
            by_column = []
            for e in range(3):
                total = None
                for b in PHASES[p][r]:
                    v = weight[b, e].astype(f32)
                    total = v if total is None else total + v
                by_column.append(total)
            for q in range(2):
                for s in range(2):
                    total = None
                    for e in PHASES[q][s]:
                        total = by_column[e] if total is None else total + by_column[e]
                    low = (2 * q + s) * channels
                    out[p, r, :, low : low + channels] = total.astype(bf16)


def planar_kernel(count, clip, counts, mid, top, bottom, kern, bias2, *rest):
    out, wide, lines, ready, sem = rest[-5:]
    rows, frames, columns, channels = mid.shape
    start = lax.axis_index("tm") * frames
    for r in range(rows + 2):
        if 0 < r <= rows:
            wide[r] = mid[r - 1]
        else:
            side = top if r == 0 else bottom
            keep = keep_row(r, rows, count, start >= 0)
            wide[r] = jnp.where(keep, side[0].astype(f32), 0.0).astype(bf16)
    copies = []
    for p in range(2):
        left = jnp.concatenate(
            [wide[p + r : p + r + rows].reshape(-1, channels) for r in range(2)], axis=1
        )
        part = jnp.dot(left, kern[p].reshape(2 * channels, 4 * channels), preferred_element_type=f32)
        for i in range(rows):
            for f in range(frames):
                n = i * frames + f
                block = part[n * columns : (n + 1) * columns]
                cut = lambda m: block[:, m * channels : (m + 1) * channels]
                even = cut(1) + shifted(cut(0), 1)
                odd = cut(2) + shifted(cut(3), -1)
                live = start + f < counts[clip]
                for k in range(channels // LANES):
                    lanes = slice(k * LANES, (k + 1) * LANES)
                    lines[k, n, pl.ds(0, columns, stride=2), :] = even[:, lanes]
                    lines[k, n, pl.ds(1, columns, stride=2), :] = odd[:, lanes]
                    value = lines[k, n] + bias2[...].reshape(1, channels)[:, lanes]
                    ready[f, 2 * i + p, :, lanes] = jnp.where(live, value, 0.0).astype(bf16)
                copies.append(
                    pltpu.make_async_copy(
                        ready.at[f, 2 * i + p], out.at[clip, f, 2 * i + p], sem.at[f, 2 * i + p]
                    )
                )
                copies[-1].start()
    for copy in copies:
        copy.wait()


def body(
    latents, frame_counts, norm_gain, norm_bias, conv3_weight, conv3_bias, conv2_weight, conv2_bias
):
    clips, frames, rows, columns, channels = latents.shape
    count = lax.axis_size("space")
    behind = lax.axis_size("tm")
    per_count = rows * count * columns * (channels // GROUPS)
    params = lambda mib: pltpu.CompilerParams(vmem_limit_bytes=mib * MIB)
    n_edges = 1 if count == 2 else 2
    shape = jax.ShapeDtypeStruct
    cost = lambda flops, size: pl.CostEstimate(flops=int(flops), bytes_accessed=int(size), transcendentals=0)
    span = 3 * channels

    stats = pl.pallas_call(
        functools.partial(stats_kernel, count),
        out_shape=[shape((2 * clips, channels), f32)]
        + [shape((frames, rows, columns, channels), bf16)] * clips
        + [shape((clips, frames, 1, columns, channels), bf16)] * n_edges,
        in_specs=[SMEM, HBM],
        out_specs=[VMEM] * (1 + clips + n_edges),
        scratch_shapes=[pltpu.SemaphoreType.DMA((clips, frames))],
        compiler_params=params(8),
        cost_estimate=cost(1e6, 8e5),
        name="stats",
    )(frame_counts, latents)
    own, own_edges = stats[1 : 1 + clips], stats[1 + clips :]
    sums = all_sum(all_sum(stats[0], "space"), "tm")
    own_top, own_bottom = exchange(own_edges, "space")
    past = [lax.ppermute(x, "tm", [(i, i + 1) for i in range(behind - 1)]) for x in own]
    past_sides = [
        exchange([lax.dynamic_slice_in_dim(x, row, 1, axis=1) for row in edge_rows(rows, count)], "space")
        for x in past
    ]

    folded = pl.pallas_call(
        fold_kernel,
        out_shape=shape((2, 2, channels, 4 * channels), bf16),
        in_specs=[VMEM],
        out_specs=VMEM,
        compiler_params=params(16),
        cost_estimate=cost(4e7, 8e6),
        name="fold",
    )(conv2_weight)

    acc, norm, past_kern = pl.pallas_call(
        functools.partial(own_kernel, count, per_count),
        out_shape=[
            shape((frames, clips, rows, columns, channels), f32),
            shape((clips, 2, channels), f32),
            shape((6, channels, span), bf16),
        ],
        in_specs=[SMEM] + [VMEM] * (5 + clips) + [HBM],
        out_specs=[VMEM] * 3,
        scratch_shapes=[
            pltpu.VMEM((frames, rows + 2, clips, columns, channels), bf16),
            pltpu.VMEM((3, channels, span), bf16),
            pltpu.SemaphoreType.DMA((3, 3)),
        ],
        compiler_params=params(24),
        cost_estimate=cost(2e9, 1e7),
        name="own",
    )(frame_counts, sums, norm_gain, norm_bias, *own, own_top, own_bottom, conv3_weight)

    out = None
    blocks = []
    for c in range(clips):
        blocks.append(
            pl.pallas_call(
                functools.partial(past_kernel, count, c),
                out_shape=[shape((rows, frames, columns, channels), bf16)]
                + [shape((1, frames, columns, channels), bf16)] * n_edges,
                in_specs=[SMEM] + [VMEM] * 8,
                out_specs=[VMEM] * (1 + n_edges),
                scratch_shapes=[pltpu.VMEM((2, rows + 2, columns, channels), bf16)],
                compiler_params=params(16),
                cost_estimate=cost(1e9, 6e6),
                name=f"past{c}",
            )(frame_counts, norm, conv3_bias, acc, past_kern, own[c], past[c], *past_sides[c])
        )
    for c in range(clips):
        mid = blocks[c][0]
        top, bottom = exchange(blocks[c][1:], "space")
        out = pl.pallas_call(
            functools.partial(planar_kernel, count, c),
            out_shape=shape((clips, frames, 2 * rows, 2 * columns, channels), bf16),
            in_specs=[SMEM] + [VMEM] * 5 + ([HBM] if c else []),
            out_specs=HBM,
            scratch_shapes=[
                pltpu.VMEM((rows + 2, frames, columns, channels), bf16),
                pltpu.VMEM((channels // LANES, rows * frames, 2 * columns, LANES), f32),
                pltpu.VMEM((frames, 2 * rows, 2 * columns, channels), bf16),
                pltpu.SemaphoreType.DMA((frames, 2 * rows)),
            ],
            input_output_aliases={6: 0} if c else {},
            compiler_params=params(16),
            cost_estimate=cost(1.3e9, 6e6),
            name=f"planar{c}",
        )(frame_counts, mid, top, bottom, folded, conv2_bias, *([out] if c else []))
    return out


def solution(mesh):
    placed = (P("clip", "tm", "space", None, None), P("clip"), P(), P(), P(), P(), P(), P())
    return jax.shard_map(
        body,
        mesh=mesh,
        in_specs=placed,
        out_specs=P("clip", "tm", "space", None, None),
        check_vma=False,
    )
```

time: 91.5 us -> 43.9 us (0.48)
  blocking collectives: 18.1 us -> 0 us
  Pallas kernels: 0 us -> 17.2 us
  matrix products: 15.1 us -> 0 us
  waiting for transfers between devices: 19.2 us -> 5.29 us
  local copies, waits for them, and re-layouts: 18.8 us -> 6.98 us
  other arithmetic: 10.4 us -> 0.01 us
  starting transfers between devices: 6.85 us -> 13.9 us
  between operations: 1.52 us -> 0.16 us
  loops' own time: 1.11 us -> 0 us
    psum x1 -> x0, blocking collectives: 18.1 us -> none  [body(): total_first, total_second = lax.psum((first, second), ('tm', 'space'))]
    pallas_call x0 -> x7, Pallas kernels: none -> 17.2 us  [the longest x2 5.72 us: body(): pl.pallas_call(functools.partial(planar_kernel, count, c), out_shape=shap...]
    conv_general_dilated x4 -> x0, matrix products: 15.1 us -> none  [the longest x2 8.39 us: planar_section(): lax.conv_general_dilated(flat, conv2_weight, (1, 1), ((0, 0), (1, 1)), di...]
    ppermute x5 -> x10, waiting for transfers between devices: 19.2 us -> 5.29 us  [the longest x3 5.28 us: all_sum(): lax.ppermute(value, axis, [(i, i ^ step) for i in range(count)])]
    ppermute x5 -> x10, starting transfers between devices: 6.85 us -> 13.9 us  [the longest x2 8.45 us: body(): lax.ppermute(x, 'tm', [(i, i + 1) for i in range(behind - 1)])]
    unnamed x11 -> x20, local copies, waits for them, and re-layouts: 0.17 us -> 6.95 us
    another operation x6 -> x0, local copies, waits for them, and re-layouts: 3.8 us -> none
    reshape x4 -> x0, local copies, waits for them, and re-layouts: 3.51 us -> none  [planar_section(): upsampled.reshape(count * frames_dev, 2 * rows_dev + 2, 2 * columns, chan...]
  transfers between devices with their start and end apart: 5 -> 10, of which waited for: 3 -> 3; matrix products, arithmetic and copies ran while one was open for 1% -> 0% of each run, Pallas kernels for 0% -> 30%
where the time goes in v2:
time: 43.9 us; the launch traced here: 43.6 us
  Pallas kernels  17.2 us (39%)
  starting transfers between devices  13.9 us (32%)
  local copies, waits for them, and re-layouts  6.98 us (16%)
  waiting for transfers between devices  5.29 us (12%)
    ppermute x2, starting transfers between devices, body(): lax.ppermute(x, 'tm', [(i, i + 1) for i in range(behind - 1)])  8.45 us
    unnamed x20, local copies, waits for them, and re-layouts  6.95 us
    pallas_call x2, Pallas kernels, body(): pl.pallas_call(functools.partial(planar_kernel, count, c), out_shape=shap...  5.72 us
    ppermute x3, waiting for transfers between devices, all_sum(): lax.ppermute(value, axis, [(i, i ^ step) for i in range(count)])  5.28 us
    pallas_call x1, Pallas kernels, body(): pl.pallas_call(functools.partial(own_kernel, count, per_count), out_shape...  4.81 us
    ppermute x3, starting transfers between devices, all_sum(): lax.ppermute(value, axis, [(i, i ^ step) for i in range(count)])  4.23 us
    pallas_call x2, Pallas kernels, body(): pl.pallas_call(functools.partial(past_kernel, count, c), out_shape=[shape...  4.2 us
    pallas_call x1, Pallas kernels, body(): pl.pallas_call(functools.partial(stats_kernel, count), out_shape=[shape((...  1.45 us
  transfers between devices with their start and end apart: 10, of which 3 were waited for; matrix products, arithmetic and copies ran while one was open for 0% of the time, Pallas kernels for 30%

profile of v2, /device:TPU:0, one launch (start us, length us, event | category | flops | bytes accessed | tf_op | source)
XLA Modules:
  0.0 43.6 jit_solution(10189377390154423596)
XLA Ops:
  0.0 1.0 %copy-done.2 = bf16[2,2,2,64,384]{4,3,2,1,0:T(8,128)(2,1)S(1)} copy-done((bf16[2,2,2,64,384]{4,3,2,1,0:T(8,128)(2,1)S(1)}, bf16[2,2,2,64,384]{4,3,2,1,0:T(8,128)(2,1)}, u32[]{:S(2)}) %copy-start.2) | copy-done | bytes 393240
  1.0 0.7 %copy-done.3 = s32[2]{0:T(128)S(1)} copy-done((s32[2]{0:T(128)S(1)}, s32[2]{0:T(128)}, u32[]{:S(2)}) %copy-start.3) | copy-done | bytes 32
  1.7 1.4 %stats.1 = (f32[4,384]{1,0:T(4,128)S(1)}, bf16[2,2,64,384]{3,2,1,0:T(8,128)(2,1)S(1)}, bf16[2,2,64,384]{3,2,1,0:T(8,128)(2,1)S(1)}, bf16[2,2,1,64,384]{4,3,2,1,0:T(8,128)(2,1)S(1)}) custom-call(s32[2]{0:T(128)S(1)} %copy-done.3, bf16[2,2,2,64,384]{4,3,2,1,0:T(8,128)(2,1)S(1)} %copy-done.2), custom_call_target="tpu_custom_call" | custom-call | flops 1000000 | bytes 800000 | tf_op jit(solution)/shard_map/stats/pallas_call | solution.py:302
  3.1 5.0 %collective-permute-start.4 = (bf16[2,2,64,384]{3,2,1,0:T(8,128)(2,1)S(1)}, bf16[2,2,64,384]{3,2,1,0:T(8,128)(2,1)S(1)}, u32[]{:S(2)}, u32[]{:S(2)}) collective-permute-start(bf16[2,2,64,384]{3,2,1,0:T(8,128)(2,1)S(1)} %get-tuple-element.18.rest_1_.own), channel_id=1, source_target_pairs={{0,2},{2,4},{4,6},{1,3},{3,5},{5,7},{8,10},{10,12},{12,14},{9,11},... | collective-permute-start | bytes 589832 | tf_op jit(solution)/shard_map/ppermute | solution.py:317
  8.1 3.5 %collective-permute-start.7 = (bf16[2,2,64,384]{3,2,1,0:T(8,128)(2,1)S(1)}, bf16[2,2,64,384]{3,2,1,0:T(8,128)(2,1)S(1)}, u32[]{:S(2)}, u32[]{:S(2)}) collective-permute-start(bf16[2,2,64,384]{3,2,1,0:T(8,128)(2,1)S(1)} %get-tuple-element.17.rest_0_.own), channel_id=1, source_target_pairs={{0,2},{2,4},{4,6},{1,3},{3,5},{5,7},{8,10},{10,12},{12,14},{9,11},... | collective-permute-start | bytes 589832 | tf_op jit(solution)/shard_map/ppermute | solution.py:317
  11.6 0.1 collective-permute-start
  11.7 1.2 %collective-permute-done = f32[4,384]{1,0:T(4,128)S(1)} collective-permute-done((f32[4,384]{1,0:T(4,128)S(1)}, f32[4,384]{1,0:T(4,128)S(1)}, u32[]{:S(2)}, u32[]{:S(2)}) %collective-permute-start) | collective-permute-done | bytes 6176 | tf_op jit(solution)/shard_map/ppermute | solution.py:44
  12.8 1.6 %collective-permute-start.1 = (f32[4,384]{1,0:T(4,128)S(1)}, f32[4,384]{1,0:T(4,128)S(1)}, u32[]{:S(2)}, u32[]{:S(2)}) collective-permute-start(f32[4,384]{1,0:T(4,128)S(1)} %add.11), channel_id=1, source_target_pairs={{0,2},{2,0},{4,6},{6,4},{1,3},{3,1},{5,7},{7,5},{8,10},{10,8},{12,... | collective-permute-start | bytes 18440 | tf_op jit(solution)/shard_map/ppermute | solution.py:44
  14.4 2.2 %collective-permute-done.1 = f32[4,384]{1,0:T(4,128)S(1)} collective-permute-done((f32[4,384]{1,0:T(4,128)S(1)}, f32[4,384]{1,0:T(4,128)S(1)}, u32[]{:S(2)}, u32[]{:S(2)}) %collective-permute-start.1) | collective-permute-done | bytes 6176 | tf_op jit(solution)/shard_map/ppermute | solution.py:44
  16.6 2.6 %collective-permute-start.2 = (f32[4,384]{1,0:T(4,128)S(1)}, f32[4,384]{1,0:T(4,128)S(1)}, u32[]{:S(2)}, u32[]{:S(2)}) collective-permute-start(f32[4,384]{1,0:T(4,128)S(1)} %add.12), channel_id=1, source_target_pairs={{0,4},{2,6},{4,0},{6,2},{1,5},{3,7},{5,1},{7,3},{8,12},{10,14},{12... | collective-permute-start | bytes 18440 | tf_op jit(solution)/shard_map/ppermute | solution.py:44
  19.2 0.0 collective-permute-start.3
  19.2 1.9 %collective-permute-done.2 = f32[4,384]{1,0:T(4,128)S(1)} collective-permute-done((f32[4,384]{1,0:T(4,128)S(1)}, f32[4,384]{1,0:T(4,128)S(1)}, u32[]{:S(2)}, u32[]{:S(2)}) %collective-permute-start.2) | collective-permute-done | bytes 6176 | tf_op jit(solution)/shard_map/ppermute | solution.py:44
  21.1 0.0 collective-permute-done.4.past
  21.1 0.1 collective-permute-start.5
  21.2 0.5 %collective-permute-start.8 = (bf16[2,1,64,384]{3,2,1,0:T(8,128)(2,1)S(1)}, bf16[2,1,64,384]{3,2,1,0:T(8,128)(2,1)S(1)}, u32[]{:S(2)}, u32[]{:S(2)}) collective-permute-start(bf16[2,1,64,384]{3,2,1,0:T(8,128)(2,1)S(1)} %constant_dynamic-slice_fusion), channel_id=1, source_target_pairs={{0,1},{1,0},{2,3},{3,2},{4,5},{5,4},{6,7},{7,6},{8,9},{9,8},{10,11... | collective-permute-start | bytes 294920 | tf_op jit(solution)/shard_map/ppermute | solution.py:30
  21.8 0.0 collective-permute-done.3.rest_2_.rest_3_
  21.8 3.3 %copy-done = bf16[3,3,3,384,384]{4,3,2,1,0:T(8,128)(2,1)S(1)} copy-done((bf16[3,3,3,384,384]{4,3,2,1,0:T(8,128)(2,1)S(1)}, bf16[3,3,3,384,384]{4,3,2,1,0:T(8,128)(2,1)}, u32[]{:S(2)}) %copy-start) | copy-done | bytes 7962648
  25.1 0.7 %copy-done.4 = s32[2]{0:T(128)S(1)} copy-done((s32[2]{0:T(128)S(1)}, s32[2]{0:T(128)}, u32[]{:S(2)}) %copy-start.4) | copy-done | bytes 32
  25.7 0.7 %copy-done.8 = f32[384]{0:T(512)S(1)} copy-done((f32[384]{0:T(512)S(1)}, f32[384]{0:T(512)}, u32[]{:S(2)}) %copy-start.8) | copy-done | bytes 1560
  26.4 0.7 %copy-done.9 = f32[384]{0:T(512)S(1)} copy-done((f32[384]{0:T(512)S(1)}, f32[384]{0:T(512)}, u32[]{:S(2)}) %copy-start.9) | copy-done | bytes 1560
  27.1 4.8 %own.1 = (f32[2,2,2,64,384]{4,3,2,1,0:T(8,128)S(1)}, f32[2,2,384]{2,1,0:T(2,128)S(1)}, bf16[6,384,1152]{2,1,0:T(8,128)(2,1)S(1)}) custom-call(s32[2]{0:T(128)S(1)} %copy-done.4, f32[4,384]{1,0:T(4,128)S(1)} %add.13.sums, f32[384]{0:T(512)S(1)} %copy-done.8, f32[384]{0:T(512)S(1)} %copy-done.9, bf16[2,2,64,384]{3,2,1,0:T(8,128)(2,1)S(1)} %get-tuple-element.17.rest_0_.own, ...), custom_call_target="tpu_custom_call" | custom-call | flops 2000000000 | bytes 10000000 | tf_op jit(solution)/shard_map/own/pallas_call | solution.py:333
  31.9 0.0 copy-start.1
  31.9 0.0 collective-permute-done.8.top.bottom
  31.9 2.1 %past0.1 = (bf16[2,2,64,384]{3,2,1,0:T(8,128)(2,1)S(1)}, bf16[1,2,64,384]{3,2,1,0:T(8,128)(2,1)S(1)}) custom-call(s32[2]{0:T(128)S(1)} %copy-done.4, f32[2,2,384]{2,1,0:T(2,128)S(1)} %get-tuple-element.20.norm, f32[384]{0:T(512)S(1)} %copy-done.7, f32[2,2,2,64,384]{4,3,2,1,0:T(8,128)S(1)} %get-tuple-element.21.acc, ...), custom_call_target="tpu_custom_call" | custom-call | flops 1000000000 | bytes 6000000 | tf_op jit(solution)/shard_map/past0/pallas_call | solution.py:356
  34.0 0.0 copy-start.5
  34.0 0.1 collective-permute-start.9
  34.1 1.0 %fold.1.kern = bf16[2,2,384,1536]{3,2,1,0:T(8,128)(2,1)S(1)} custom-call(bf16[3,3,384,384]{3,2,1,0:T(8,128)(2,1)S(1)} %copy-done.1), custom_call_target="tpu_custom_call" | custom-call | flops 40000000 | bytes 8000000 | tf_op jit(solution)/shard_map/fold/pallas_call | solution.py:323
  35.2 0.0 copy-start.6
  35.2 2.1 %past1.1 = (bf16[2,2,64,384]{3,2,1,0:T(8,128)(2,1)S(1)}, bf16[1,2,64,384]{3,2,1,0:T(8,128)(2,1)S(1)}) custom-call(s32[2]{0:T(128)S(1)} %copy-done.5, f32[2,2,384]{2,1,0:T(2,128)S(1)} %get-tuple-element.20.norm, f32[384]{0:T(512)S(1)} %copy-done.7, f32[2,2,2,64,384]{4,3,2,1,0:T(8,128)S(1)} %get-tuple-element.21.acc, ...), custom_call_target="tpu_custom_call" | custom-call | flops 1000000000 | bytes 6000000 | tf_op jit(solution)/shard_map/past1/pallas_call | solution.py:356
  37.3 0.5 %collective-permute-start.6 = (bf16[1,2,64,384]{3,2,1,0:T(8,128)(2,1)S(1)}, bf16[1,2,64,384]{3,2,1,0:T(8,128)(2,1)S(1)}, u32[]{:S(2)}, u32[]{:S(2)}) collective-permute-start(bf16[1,2,64,384]{3,2,1,0:T(8,128)(2,1)S(1)} %get-tuple-element.24), channel_id=1, source_target_pairs={{0,1},{1,0},{2,3},{3,2},{4,5},{5,4},{6,7},{7,6},{8,9},{9,8},{10,11... | collective-permute-start | bytes 294920 | tf_op jit(solution)/shard_map/ppermute | solution.py:30
  37.8 2.9 %planar0.1.rest_0_ = bf16[2,2,4,128,384]{4,3,2,1,0:T(8,128)(2,1)} custom-call(s32[2]{0:T(128)S(1)} %copy-done.5, bf16[2,2,64,384]{3,2,1,0:T(8,128)(2,1)S(1)} %get-tuple-element.25.mid, bf16[1,2,64,384]{3,2,1,0:T(8,128)(2,1)S(1)} %collective-permute-done.9.top.bottom, bf16[1,2,64,384]{3,2,1,0:T(8,128)(2,1)S(1)} %collective-permute-done.9.top.bottom, ...), custom_call_target="tpu_custom_call" | custom-call | flops 1300000000 | bytes 6000000 | tf_op jit(solution)/shard_map/planar0/pallas_call | solution.py:371
  40.7 2.9 %planar1.1 = bf16[2,2,4,128,384]{4,3,2,1,0:T(8,128)(2,1)} custom-call(s32[2]{0:T(128)S(1)} %copy-done.5, bf16[2,2,64,384]{3,2,1,0:T(8,128)(2,1)S(1)} %get-tuple-element.23.mid, bf16[1,2,64,384]{3,2,1,0:T(8,128)(2,1)S(1)} %collective-permute-done.6.top.bottom, ...), custom_call_target="tpu_custom_call", output_to_operand_aliasing={{}: (6, {})} | custom-call | flops 1300000000 | bytes 6000000 | tf_op jit(solution)/shard_map/planar1/pallas_call | solution.py:371
  (20 shorter events, 0.1 us)
Async XLA Ops:
  0.0 1.0 %copy-start.2 = (bf16[2,2,2,64,384]{4,3,2,1,0:T(8,128)(2,1)S(1)}, bf16[2,2,2,64,384]{4,3,2,1,0:T(8,128)(2,1)}, u32[]{:S(2)}) copy-start(bf16[2,2,2,64,384]{4,3,2,1,0:T(8,128)(2,1)} %x.1) | copy-start | bytes 1179652
  1.0 0.7 %copy-start.3 = (s32[2]{0:T(128)S(1)}, s32[2]{0:T(128)}, u32[]{:S(2)}) copy-start(s32[2]{0:T(128)} %counts.11) | copy-start | bytes 28
  1.7 30.3 %copy-start.7 = (f32[384]{0:T(512)S(1)}, f32[384]{0:T(512)}, u32[]{:S(2)}) copy-start(f32[384]{0:T(512)} %bias3.3) | copy-start | bytes 4612
  3.1 18.0 %collective-permute-start.4 = (bf16[2,2,64,384]{3,2,1,0:T(8,128)(2,1)S(1)}, bf16[2,2,64,384]{3,2,1,0:T(8,128)(2,1)S(1)}, u32[]{:S(2)}, u32[]{:S(2)}) collective-permute-start(bf16[2,2,64,384]{3,2,1,0:T(8,128)(2,1)S(1)} %get-tuple-element.18.rest_1_.own), channel_id=1, source_target_pairs={{0,2},{2,4},{4,6},{1,3},{3,5},{5,7},{8,10},{10,12},{12,14},{9,11},... | collective-permute-start | bytes 589832 | tf_op jit(solution)/shard_map/ppermute | solution.py:317
  8.1 13.1 %collective-permute-start.7 = (bf16[2,2,64,384]{3,2,1,0:T(8,128)(2,1)S(1)}, bf16[2,2,64,384]{3,2,1,0:T(8,128)(2,1)S(1)}, u32[]{:S(2)}, u32[]{:S(2)}) collective-permute-start(bf16[2,2,64,384]{3,2,1,0:T(8,128)(2,1)S(1)} %get-tuple-element.17.rest_0_.own), channel_id=1, source_target_pairs={{0,2},{2,4},{4,6},{1,3},{3,5},{5,7},{8,10},{10,12},{12,14},{9,11},... | collective-permute-start | bytes 589832 | tf_op jit(solution)/shard_map/ppermute | solution.py:317
  11.6 1.2 %collective-permute-start = (f32[4,384]{1,0:T(4,128)S(1)}, f32[4,384]{1,0:T(4,128)S(1)}, u32[]{:S(2)}, u32[]{:S(2)}) collective-permute-start(f32[4,384]{1,0:T(4,128)S(1)} %get-tuple-element.16), channel_id=1, source_target_pairs={{0,1},{1,0},{2,3},{3,2},{4,5},{5,4},{6,7},{7,6},{8,9},{9,8},{10,11... | collective-permute-start | bytes 18440 | tf_op jit(solution)/shard_map/ppermute | solution.py:44
  12.8 3.7 %collective-permute-start.1 = (f32[4,384]{1,0:T(4,128)S(1)}, f32[4,384]{1,0:T(4,128)S(1)}, u32[]{:S(2)}, u32[]{:S(2)}) collective-permute-start(f32[4,384]{1,0:T(4,128)S(1)} %add.11), channel_id=1, source_target_pairs={{0,2},{2,0},{4,6},{6,4},{1,3},{3,1},{5,7},{7,5},{8,10},{10,8},{12,... | collective-permute-start | bytes 18440 | tf_op jit(solution)/shard_map/ppermute | solution.py:44
  16.6 4.5 %collective-permute-start.2 = (f32[4,384]{1,0:T(4,128)S(1)}, f32[4,384]{1,0:T(4,128)S(1)}, u32[]{:S(2)}, u32[]{:S(2)}) collective-permute-start(f32[4,384]{1,0:T(4,128)S(1)} %add.12), channel_id=1, source_target_pairs={{0,4},{2,6},{4,0},{6,2},{1,5},{3,7},{5,1},{7,3},{8,12},{10,14},{12... | collective-permute-start | bytes 18440 | tf_op jit(solution)/shard_map/ppermute | solution.py:44
  19.2 2.6 %collective-permute-start.3 = (bf16[2,2,1,64,384]{4,3,2,1,0:T(8,128)(2,1)S(1)}, bf16[2,2,1,64,384]{4,3,2,1,0:T(8,128)(2,1)S(1)}, u32[]{:S(2)}, u32[]{:S(2)}) collective-permute-start(bf16[2,2,1,64,384]{4,3,2,1,0:T(8,128)(2,1)S(1)} %get-tuple-element.19), channel_id=1, source_target_pairs={{0,1},{1,0},{2,3},{3,2},{4,5},{5,4},{6,7},{7,6},{8,9},{9,8},{10,11... | collective-permute-start | bytes 589832 | tf_op jit(solution)/shard_map/ppermute | solution.py:30
  21.1 14.0 %collective-permute-start.5 = (bf16[2,1,64,384]{3,2,1,0:T(8,128)(2,1)S(1)}, bf16[2,1,64,384]{3,2,1,0:T(8,128)(2,1)S(1)}, u32[]{:S(2)}, u32[]{:S(2)}) collective-permute-start(bf16[2,1,64,384]{3,2,1,0:T(8,128)(2,1)S(1)} %constant_dynamic-slice_fusion.1), channel_id=1, source_target_pairs={{0,1},{1,0},{2,3},{3,2},{4,5},{5,4},{6,7},{7,6},{8,9},{9,8},{10,11... | collective-permute-start | bytes 294920 | tf_op jit(solution)/shard_map/ppermute | solution.py:30
  21.2 10.7 %collective-permute-start.8 = (bf16[2,1,64,384]{3,2,1,0:T(8,128)(2,1)S(1)}, bf16[2,1,64,384]{3,2,1,0:T(8,128)(2,1)S(1)}, u32[]{:S(2)}, u32[]{:S(2)}) collective-permute-start(bf16[2,1,64,384]{3,2,1,0:T(8,128)(2,1)S(1)} %constant_dynamic-slice_fusion), channel_id=1, source_target_pairs={{0,1},{1,0},{2,3},{3,2},{4,5},{5,4},{6,7},{7,6},{8,9},{9,8},{10,11... | collective-permute-start | bytes 294920 | tf_op jit(solution)/shard_map/ppermute | solution.py:30
  21.8 3.3 %copy-start = (bf16[3,3,3,384,384]{4,3,2,1,0:T(8,128)(2,1)S(1)}, bf16[3,3,3,384,384]{4,3,2,1,0:T(8,128)(2,1)}, u32[]{:S(2)}) copy-start(bf16[3,3,3,384,384]{4,3,2,1,0:T(8,128)(2,1)} %rest_4_.1) | copy-start | bytes 23887876
  25.1 0.7 %copy-start.4 = (s32[2]{0:T(128)S(1)}, s32[2]{0:T(128)}, u32[]{:S(2)}) copy-start(s32[2]{0:T(128)} %counts.11) | copy-start | bytes 28
  25.7 0.7 %copy-start.8 = (f32[384]{0:T(512)S(1)}, f32[384]{0:T(512)}, u32[]{:S(2)}) copy-start(f32[384]{0:T(512)} %gain.1) | copy-start | bytes 4612
  26.4 0.7 %copy-start.9 = (f32[384]{0:T(512)S(1)}, f32[384]{0:T(512)}, u32[]{:S(2)}) copy-start(f32[384]{0:T(512)} %bias.1) | copy-start | bytes 4612
  31.9 2.2 %copy-start.1 = (bf16[3,3,384,384]{3,2,1,0:T(8,128)(2,1)S(1)}, bf16[3,3,384,384]{3,2,1,0:T(8,128)(2,1)}, u32[]{:S(2)}) copy-start(bf16[3,3,384,384]{3,2,1,0:T(8,128)(2,1)} %weight.1) | copy-start | bytes 7962628
  34.0 1.2 %copy-start.5 = (s32[2]{0:T(128)S(1)}, s32[2]{0:T(128)}, u32[]{:S(2)}) copy-start(s32[2]{0:T(128)} %counts.11) | copy-start | bytes 28
  34.0 3.8 %collective-permute-start.9 = (bf16[1,2,64,384]{3,2,1,0:T(8,128)(2,1)S(1)}, bf16[1,2,64,384]{3,2,1,0:T(8,128)(2,1)S(1)}, u32[]{:S(2)}, u32[]{:S(2)}) collective-permute-start(bf16[1,2,64,384]{3,2,1,0:T(8,128)(2,1)S(1)} %get-tuple-element.26), channel_id=1, source_target_pairs={{0,1},{1,0},{2,3},{3,2},{4,5},{5,4},{6,7},{7,6},{8,9},{9,8},{10,11... | collective-permute-start | bytes 294920 | tf_op jit(solution)/shard_map/ppermute | solution.py:30
  35.2 2.7 %copy-start.6 = (f32[384]{0:T(512)S(1)}, f32[384]{0:T(512)}, u32[]{:S(2)}) copy-start(f32[384]{0:T(512)} %bias2.3) | copy-start | bytes 4612
  37.3 3.4 %collective-permute-start.6 = (bf16[1,2,64,384]{3,2,1,0:T(8,128)(2,1)S(1)}, bf16[1,2,64,384]{3,2,1,0:T(8,128)(2,1)S(1)}, u32[]{:S(2)}, u32[]{:S(2)}) collective-permute-start(bf16[1,2,64,384]{3,2,1,0:T(8,128)(2,1)S(1)} %get-tuple-element.24), channel_id=1, source_target_pairs={{0,1},{1,0},{2,3},{3,2},{4,5},{5,4},{6,7},{7,6},{8,9},{9,8},{10,11... | collective-permute-start | bytes 294920 | tf_op jit(solution)/shard_map/ppermute | solution.py:30
